TPU v7x, 128 devices: a whole 4x4x4 slice. The times are simulated.
128 devices in a mesh: el: 8 (over x, core), tg: 16 (over y, z).
Axes of the slice: x: 4, y: 4, z: 4, core: 2. Of those that a mesh axis runs over, the one named last changes fastest.
Arguments:
- field_points: bfloat16 [65536, 16, 256], P(('el', 'tg')), may hold values from -6 to 6
- owner_map: int32 [128, 512], P(('el', 'tg')), may hold values from 0 to 127, as said below
- send_counts: int32 [128, 512], P(('el', 'tg')), may hold values from 15 to 16
- tile_rows: int32 [128, 32], P(('el', 'tg')), may hold values from 0 to 31, each once within a row
- tile_cols: int32 [128, 32, 16], P(('el', 'tg')), may hold values from 0 to 63, as said below
- weights: bfloat16 [128, 32, 16, 128, 128], P(('el', 'tg')), may hold values from -0.125 to 0.125
Outputs:
- remapped: bfloat16 [256, 524288], P('el', 'tg')
Inputs may be any that keep to these rules, and one draw needn't show every extreme that they name: `owner_map`: each device's 512 elements name every owner exactly 4 times. `tile_cols`: the 16 entries of one target tile are distinct.
All inputs are finite; a program needn't handle non-finite values.
Results may differ from a plain program's by a relative error of at most 0.001.
Values may be sent and summed in bfloat16 or wider, within the bound.
No kernel may reach another device: no remote copies, remote signals or barrier semaphores. Data moves between devices by JAX's collectives and lax.ppermute only.
A program may use at most 128 MiB of HBM per device.

v0:
```python
import jax
import jax.numpy as jnp
from jax import lax
from jax.sharding import PartitionSpec as P


def on_device(field_points, owner_map, send_counts, tile_rows, tile_cols, weights):
    elem_count, point_count, channels = field_points.shape
    devices = lax.axis_size(("el", "tg"))
    per_owner = elem_count // devices
    ordering = jnp.argsort(owner_map[0], stable=True)
    packed = field_points[ordering]
    counts_sorted = send_counts[0][ordering]
    point_index = lax.broadcasted_iota(jnp.int32, (elem_count, point_count), 1)
    live_rows = point_index < counts_sorted[:, None]
    packed = jnp.where(live_rows[:, :, None], packed, jnp.zeros((), packed.dtype))
    outgoing = packed.reshape(devices, per_owner * point_count, channels)
    incoming = lax.all_to_all(outgoing, ("el", "tg"), split_axis=0, concat_axis=0, tiled=True)
    tile_width = weights.shape[-1]
    source = incoming.reshape(-1, tile_width, channels)
    gathered = source[tile_cols[0]]
    product = jnp.einsum("tkij,tkjc->cti", weights[0], gathered, preferred_element_type=jnp.float32)
    placed = jnp.zeros_like(product).at[:, tile_rows[0]].set(product)
    merged = placed.reshape(channels, -1).astype(jnp.bfloat16)
    return lax.all_to_all(merged, "el", split_axis=0, concat_axis=1, tiled=True)


def solution(mesh):
    return jax.shard_map(
        on_device,
        mesh=mesh,
        in_specs=(
            P(("el", "tg"), None, None),
            P(("el", "tg"), None),
            P(("el", "tg"), None),
            P(("el", "tg"), None),
            P(("el", "tg"), None, None),
            P(("el", "tg"), None, None, None, None),
        ),
        out_specs=P("el", "tg"),
        check_vma=False,
    )
```

profile of v0, /device:TPU:1, one launch (start us, length us, event | category | flops | bytes accessed | tf_op | source)
XLA Modules:
  0.0 171.4 jit_solution(1882623141803326845)
XLA Ops:
  0.0 4.5 %sort.17 = (s32[512]{0:T(512)}, s32[512]{0:T(512)S(1)}) sort(s32[512]{0:T(512)} %bitcast.33, s32[512]{0:T(512)S(1)} %iota.19), dimensions={0}, to_apply=%region_0.0 | sort | flops 4608 | bytes 8192 | tf_op jit(solution)/shard_map/jit(argsort)/sort | solution.py:11
  4.5 5.1 %gather_fusion.1 = bf16[512,16,256]{2,1,0:T(8,128)(2,1)} fusion(bf16[512,16,256]{2,1,0:T(8,128)(2,1)} %param.6, s32[1024]{0:T(1024)S(1)} %pad_clamp_fusion.1), kind=kCustom, calls=%fused_computation.1 | custom fusion | bytes 8390656 | tf_op jit(solution)/shard_map/gather | solution.py:12
  9.6 0.0 copy-done
  9.6 3.5 %gather_fusion = s32[512]{0:T(512)S(1)} fusion(s32[512]{0:T(512)S(1)} %bitcast.29, s32[1024]{0:T(1024)S(1)} %pad_clamp_fusion.1), kind=kCustom, calls=%fused_computation | custom fusion | bytes 6144 | tf_op jit(solution)/shard_map/gather | solution.py:13
  13.1 0.1 lt.49
  13.2 0.1 copy.12
  13.3 0.1 iota.17
  13.4 0.1 bitcast_compare_fusion
  13.5 0.1 copy.13
  13.6 5.3 %bitcast_select_fusion = bf16[128,64,256]{2,1,0:T(8,128)(2,1)} fusion(pred[128,64]{1,0:T(8,128)(4,1)S(1)} %copy.13, bf16[128,64,256]{2,1,0:T(8,128)(2,1)} %bitcast.31), kind=kLoop, calls=%fused_computation.6 | loop fusion | flops 2097152 | bytes 8396800 | tf_op jit(solution)/shard_map/jit(_where)/select_n | solution.py:16
  18.9 11.9 %all-to-all-start = ((bf16[128,64,256]{2,1,0:T(8,128)(2,1)}), bf16[128,64,256]{2,1,0:T(8,128)(2,1)}, u32[]{:S(2)}, u32[]{:S(2)}) async-start(bf16[128,64,256]{2,1,0:T(8,128)(2,1)} %bitcast_select_fusion), calls=%async_computation | async-start | bytes 8388608 | tf_op jit(solution)/shard_map/all_to_all | solution.py:18
  30.8 0.1 copy.14
  30.9 0.1 reshape.108
  31.0 51.7 %all-to-all-done = bf16[128,64,256]{2,1,0:T(8,128)(2,1)} async-done(((bf16[128,64,256]{2,1,0:T(8,128)(2,1)}), bf16[128,64,256]{2,1,0:T(8,128)(2,1)}, u32[]{:S(2)}, u32[]{:S(2)}) %all-to-all-start) | async-done | bytes 4194336 | tf_op jit(solution)/shard_map/all_to_all | solution.py:18
  82.8 18.3 %gather_fusion.2 = bf16[512,128,256]{2,1,0:T(8,128)(2,1)} fusion(bf16[64,128,256]{2,1,0:T(8,128)(2,1)} %bitcast.6, s32[1024]{0:T(1024)S(1)} %pad_clamp_fusion), kind=kCustom, calls=%fused_computation.2 | custom fusion | bytes 67110912 | tf_op jit(solution)/shard_map/gather | solution.py:21
  101.1 20.0 %fusion.2 = f32[32,256,128]{2,1,0:T(8,128)} fusion(bf16[32,16,128,256]{3,2,1,0:T(8,128)(2,1)} %bitcast.30, bf16[1,32,16,128,128]{4,3,2,1,0:T(8,128)(2,1)} %param.11), kind=kOutput, calls=%fused_computation.7 | convolution fusion | flops 4294967296 | bytes 54525952 | tf_op jit(solution)/shard_map/tkij,tkjc->cti/dot_general | solution.py:22
  121.1 2.4 %broadcast_in_dim.23 = f32[256,32,128]{2,0,1:T(8,128)} broadcast(f32[]{:T(128)} %constant.6.clone.1), dimensions={} | broadcast | bytes 4194308 | tf_op jit(solution)/shard_map/broadcast_in_dim | solution.py:23
  123.5 8.3 %scatter_fusion = f32[256,32,128]{2,0,1:T(8,128)} fusion(f32[256,32,128]{2,0,1:T(8,128)} %broadcast_in_dim.23, s32[32]{0:T(128)S(1)} %fusion.5, f32[32,256,128]{2,1,0:T(8,128)} %fusion.2), kind=kCustom, calls=%fused_computation.3 | custom fusion | bytes 12583040 | tf_op jit(solution)/shard_map/scatter | solution.py:23
  131.9 2.5 %convert_element_type.7 = bf16[256,32,128]{2,0,1:T(8,128)(2,1)S(1)} convert(f32[256,32,128]{2,0,1:T(8,128)} %scatter_fusion) | non-fusion elementwise | flops 1048576 | bytes 6291456 | tf_op jit(solution)/shard_map/convert_element_type | solution.py:24
  134.4 1.4 copy.16
  135.7 0.0 copy-start.1
  135.7 2.3 %convert_element_type.8 = bf16[8,32,4096]{2,1,0:T(8,128)(2,1)} reshape(bf16[256,32,128]{2,1,0:T(8,128)(2,1)S(1)} %copy.16) | data formatting | bytes 4194304 | tf_op jit(solution)/shard_map/convert_element_type | solution.py:24
  138.0 31.9 %all_to_all.21 = bf16[8,32,4096]{2,1,0:T(8,128)(2,1)S(1)} all-to-all(bf16[8,32,4096]{2,1,0:T(8,128)(2,1)} %convert_element_type.8), channel_id=1, replica_groups=mesh['el'=8,'tg'=16] {'el'}, dimensions={0} | all-to-all | bytes 4194304 | tf_op jit(solution)/shard_map/all_to_all | solution.py:25
  169.9 1.5 copy.20
  (13 shorter events, 0.0 us)
Async XLA Ops:
  0.0 9.6 %copy-start = (s32[1,512]{1,0:T(1,128)S(1)}, s32[1,512]{1,0:T(1,128)}, u32[]{:S(2)}) copy-start(s32[1,512]{1,0:T(1,128)} %param.8) | copy-start | bytes 6148
  18.9 12.0 %copy-start.2 = (s32[1,32,16]{1,2,0:T(8,128)S(1)}, s32[1,32,16]{1,2,0:T(8,128)}, u32[]{:S(2)}) copy-start(s32[1,32,16]{1,2,0:T(8,128)} %param.10) | copy-start | bytes 6148
  18.9 12.1 %copy-start.3 = (s32[1,32]{1,0:T(1,128)S(1)}, s32[1,32]{1,0:T(1,128)}, u32[]{:S(2)}) copy-start(s32[1,32]{1,0:T(1,128)} %param.9) | copy-start | bytes 388
  18.9 63.9 %all-to-all-start = ((bf16[128,64,256]{2,1,0:T(8,128)(2,1)}), bf16[128,64,256]{2,1,0:T(8,128)(2,1)}, u32[]{:S(2)}, u32[]{:S(2)}) async-start(bf16[128,64,256]{2,1,0:T(8,128)(2,1)} %bitcast_select_fusion), calls=%async_computation | async-start | bytes 8388608 | tf_op jit(solution)/shard_map/all_to_all | solution.py:18
  135.7 35.7 %copy-start.1 = (s32[1,512]{1,0:T(1,128)S(1)}, s32[1,512]{1,0:T(1,128)}, u32[]{:S(2)}) copy-start(s32[1,512]{1,0:T(1,128)} %param.8) | copy-start | bytes 6148
where the time goes:
time: 172 us; the launch traced here: 171 us
  waiting for transfers between devices  51.7 us (30%)
  local copies, waits for them, and re-layouts  43.3 us (25%)
  blocking collectives  31.9 us (19%)
  matrix products  20 us (12%)
  other arithmetic  12.3 us (7%)
  starting transfers between devices  11.9 us (7%)
    all_to_all x1, waiting for transfers between devices, on_device(): lax.all_to_all(outgoing, ('el', 'tg'), split_axis=0, concat_axis=0, tiled...  51.7 us
    all_to_all x1, blocking collectives, on_device(): return lax.all_to_all(merged, 'el', split_axis=0, concat_axis=1, tiled=True)  31.9 us
    dot_general x1, matrix products, on_device(): jnp.einsum('tkij,tkjc->cti', weights[0], gathered, preferred_element_type...  20 us
    gather x1, local copies, waits for them, and re-layouts, on_device(): gathered = source[tile_cols[0]]  18.3 us
    all_to_all x1, starting transfers between devices, on_device(): lax.all_to_all(outgoing, ('el', 'tg'), split_axis=0, concat_axis=0, tiled...  11.9 us
    scatter x1, local copies, waits for them, and re-layouts, on_device(): placed = jnp.zeros_like(product).at[:, tile_rows[0]].set(product)  8.34 us
    select_n x1, other arithmetic, on_device(): jnp.where(live_rows[:, :, None], packed, jnp.zeros((), packed.dtype))  5.25 us
    gather x1, local copies, waits for them, and re-layouts, on_device(): packed = field_points[ordering]  5.13 us
  transfers between devices with their start and end apart: 1, of which 1 were waited for; matrix products, arithmetic and copies ran while one was open for 0% of the time, Pallas kernels for 0%

commit v1 on v0

v1 whole, which is shorter than its diff:
```python
import functools
import jax
import jax.numpy as jnp
from jax import lax
from jax.experimental import pallas as pl
from jax.experimental.pallas import tpu as pltpu
from jax.sharding import PartitionSpec as P


def pack_kernel(chunks, owner_ref, counts_ref, field_ref, out_ref, buf, dst, pos_v, pos_s, sem_in, sem_pos, sem_out):
    elems, points, channels = dst.shape
    step = elems // chunks
    owners = elems // 4
    def fetch(c):
        return pltpu.make_async_copy(field_ref.at[pl.ds(c * step, step)], buf.at[pl.ds(c * step, step)], sem_in.at[c])
    for c in range(chunks):
        fetch(c).start()
    owner = owner_ref[...]
    hit = lax.broadcasted_iota(jnp.int32, (owners, elems), 0) == owner
    hit = jnp.where(hit, 1.0, 0.0)
    before = jnp.where(lax.broadcasted_iota(jnp.int32, (elems, elems), 0) < lax.broadcasted_iota(jnp.int32, (elems, elems), 1), 1.0, 0.0)
    earlier = jnp.dot(hit.astype(jnp.bfloat16), before.astype(jnp.bfloat16), preferred_element_type=jnp.float32)
    rank = jnp.sum(hit * earlier, axis=0, keepdims=True)
    pos_v[...] = owner * 4 + rank.astype(jnp.int32)
    cp = pltpu.make_async_copy(pos_v, pos_s, sem_pos)
    cp.start()
    cp.wait()
    point = lax.broadcasted_iota(jnp.int32, (points, channels), 0)
    for c in range(chunks):
        fetch(c).wait()
        def body(e, carry):
            live = point < counts_ref[0, e]
            dst[pos_s[0, e]] = jnp.where(live, buf[e], jnp.zeros((), buf.dtype))
            return carry
        lax.fori_loop(c * step, (c + 1) * step, body, 0, unroll=8)
    out = pltpu.make_async_copy(dst, out_ref, sem_out)
    out.start()
    out.wait()

def pack(owner_map, send_counts, field, chunks=8):
    return pl.pallas_call(
        functools.partial(pack_kernel, chunks),
        out_shape=jax.ShapeDtypeStruct(field.shape, field.dtype),
        in_specs=[pl.BlockSpec(memory_space=pltpu.VMEM), pl.BlockSpec(memory_space=pltpu.SMEM), pl.BlockSpec(memory_space=pl.ANY)],
        out_specs=pl.BlockSpec(memory_space=pl.ANY),
        scratch_shapes=[
            pltpu.VMEM(field.shape, field.dtype),
            pltpu.VMEM(field.shape, field.dtype),
            pltpu.VMEM((1, field.shape[0]), jnp.int32),
            pltpu.SMEM((1, field.shape[0]), jnp.int32),
            pltpu.SemaphoreType.DMA((chunks,)),
            pltpu.SemaphoreType.DMA,
            pltpu.SemaphoreType.DMA,
        ],
        name="pack",
    )(owner_map, send_counts, field)

def remap_kernel(rows_ref, cols_ref, w_ref, src_ref, out_ref):
    t = pl.program_id(0)
    per, blocks, tile, _ = w_ref.shape[1:]
    for u in range(per):
        tt = t * per + u
        acc = None
        for k in range(0, blocks, 2):
            w = jnp.concatenate([w_ref[0, u, k], w_ref[0, u, k + 1]], axis=1)
            s = jnp.concatenate([src_ref[cols_ref[0, tt, k]], src_ref[cols_ref[0, tt, k + 1]]], axis=0)
            p = jnp.dot(w, s, preferred_element_type=jnp.float32)
            acc = p if acc is None else acc + p
        lane = pl.multiple_of(rows_ref[0, tt] * tile, tile)
        out_ref[:, pl.ds(lane, tile)] = acc.T.astype(out_ref.dtype)

def remap(tile_rows, tile_cols, weights, source, per=1):
    _, targets, blocks, tile, _ = weights.shape
    channels = source.shape[-1]
    return pl.pallas_call(
        remap_kernel,
        out_shape=jax.ShapeDtypeStruct((channels, targets * tile), jnp.bfloat16),
        grid_spec=pltpu.PrefetchScalarGridSpec(
            num_scalar_prefetch=2,
            grid=(targets // per,),
            in_specs=[
                pl.BlockSpec((1, per, blocks, tile, tile), lambda t, *_: (0, t, 0, 0, 0)),
                pl.BlockSpec(source.shape, lambda t, *_: (0, 0, 0)),
            ],
            out_specs=pl.BlockSpec((channels, targets * tile), lambda t, *_: (0, 0)),
        ),
        name="remap",
    )(tile_rows, tile_cols, weights, source)


def on_device(field_points, owner_map, send_counts, tile_rows, tile_cols, weights):
    elems, points, channels = field_points.shape
    devices = lax.axis_size(("el", "tg"))
    packed = pack(owner_map, send_counts, field_points)
    outgoing = packed.reshape(devices, elems // devices * points, channels)
    incoming = lax.all_to_all(outgoing, ("el", "tg"), split_axis=0, concat_axis=0, tiled=True)
    source = incoming.reshape(-1, weights.shape[-1], channels)
    merged = remap(tile_rows, tile_cols, weights, source, per=8)
    return lax.all_to_all(merged, "el", split_axis=0, concat_axis=1, tiled=True)


def solution(mesh):
    return jax.shard_map(
        on_device,
        mesh=mesh,
        in_specs=(
            P(("el", "tg"), None, None),
            P(("el", "tg"), None),
            P(("el", "tg"), None),
            P(("el", "tg"), None),
            P(("el", "tg"), None, None),
            P(("el", "tg"), None, None, None, None),
        ),
        out_specs=P("el", "tg"),
        check_vma=False,
    )
```

time: 172 us -> 115 us (0.67)
  local copies, waits for them, and re-layouts: 43.3 us -> 2.15 us
  matrix products: 20 us -> 0 us
  Pallas kernels: 0 us -> 17.4 us
  other arithmetic: 12.3 us -> 0 us
    gather x3 -> x0, local copies, waits for them, and re-layouts: 26.9 us -> none  [the longest x1 18.3 us: on_device(): gathered = source[tile_cols[0]]]
    dot_general x1 -> x0, matrix products: 20 us -> none  [on_device(): jnp.einsum('tkij,tkjc->cti', weights[0], gathered, preferred_element_type...]
    pallas_call x0 -> x2, Pallas kernels: none -> 17.4 us  [the longest x1 12.3 us: remap(): pl.pallas_call(remap_kernel, out_shape=jax.ShapeDtypeStruct((channels, ta...]
    scatter x1 -> x0, local copies, waits for them, and re-layouts: 8.34 us -> none  [on_device(): placed = jnp.zeros_like(product).at[:, tile_rows[0]].set(product)]
    select_n x4 -> x0, other arithmetic: 5.27 us -> none  [the longest x1 5.25 us: on_device(): jnp.where(live_rows[:, :, None], packed, jnp.zeros((), packed.dtype))]
    sort x1 -> x0, other arithmetic: 4.45 us -> none  [on_device(): ordering = jnp.argsort(owner_map[0], stable=True)]
    convert_element_type x2 -> x0, local copies, waits for them, and re-layouts: 3.65 us -> none  [on_device(): merged = placed.reshape(channels, -1).astype(jnp.bfloat16)]
    convert_element_type x1 -> x0, other arithmetic: 2.51 us -> none  [on_device(): merged = placed.reshape(channels, -1).astype(jnp.bfloat16)]
  transfers between devices with their start and end apart: 1 -> 1, of which waited for: 1 -> 1; matrix products, arithmetic and copies ran while one was open for 0% -> 1% of each run, Pallas kernels for 0% -> 0%
where the time goes in v1:
time: 115 us
  waiting for transfers between devices  51.2 us (45%)
  blocking collectives  32 us (28%)
  Pallas kernels  17.4 us (15%)
  starting transfers between devices  12 us (10%)
  local copies, waits for them, and re-layouts  2.15 us (2%)
    all_to_all x1, waiting for transfers between devices, on_device(): lax.all_to_all(outgoing, ('el', 'tg'), split_axis=0, concat_axis=0, tiled...  51.2 us
    all_to_all x1, blocking collectives, on_device(): return lax.all_to_all(merged, 'el', split_axis=0, concat_axis=1, tiled=True)  32 us
    pallas_call x1, Pallas kernels, remap(): pl.pallas_call(remap_kernel, out_shape=jax.ShapeDtypeStruct((channels, ta...  12.3 us
    all_to_all x1, starting transfers between devices, on_device(): lax.all_to_all(outgoing, ('el', 'tg'), split_axis=0, concat_axis=0, tiled...  12 us
    pallas_call x1, Pallas kernels, pack(): pl.pallas_call(functools.partial(pack_kernel, chunks), out_shape=jax.Shap...  5.15 us
  transfers between devices with their start and end apart: 1, of which 1 were waited for; matrix products, arithmetic and copies ran while one was open for 1% of the time, Pallas kernels for 0%

profile of v1, /device:TPU:1, one launch (start us, length us, event | category | flops | bytes accessed | tf_op | source)
XLA Modules:
  0.0 114.8 jit_solution(13994325411659193411)
XLA Ops:
  0.0 5.1 %pack.1 = bf16[512,16,256]{2,1,0:T(8,128)(2,1)} custom-call(s32[1,512]{1,0:T(1,128)} %owner_ref.1, s32[1,512]{1,0:T(1,128)} %counts_ref.1, bf16[512,16,256]{2,1,0:T(8,128)(2,1)} %field_ref.1), custom_call_target="tpu_custom_call" | custom-call | tf_op jit(solution)/shard_map/pack/pallas_call | solution.py:41
  5.2 0.0 copy-start
  5.2 12.0 %all-to-all-start = ((bf16[128,64,256]{2,1,0:T(8,128)(2,1)}), bf16[128,64,256]{2,1,0:T(8,128)(2,1)}, u32[]{:S(2)}, u32[]{:S(2)}) async-start(bf16[128,64,256]{2,1,0:T(8,128)(2,1)} %bitcast.6), calls=%async_computation | async-start | bytes 8388608 | tf_op jit(solution)/shard_map/all_to_all | solution.py:96
  17.1 0.0 copy-done
  17.1 0.7 copy.7.cols_ref
  17.8 51.2 %all-to-all-done = bf16[128,64,256]{2,1,0:T(8,128)(2,1)} async-done(((bf16[128,64,256]{2,1,0:T(8,128)(2,1)}), bf16[128,64,256]{2,1,0:T(8,128)(2,1)}, u32[]{:S(2)}, u32[]{:S(2)}) %all-to-all-start) | async-done | bytes 4194336 | tf_op jit(solution)/shard_map/all_to_all | solution.py:96
  69.1 12.3 %remap.1 = bf16[256,4096]{1,0:T(8,128)(2,1)} custom-call(s32[1,32]{1,0:T(1,128)} %rows_ref.1, s32[1,32,16]{2,1,0:T(8,128)} %copy.7.cols_ref, bf16[1,32,16,128,128]{4,3,2,1,0:T(8,128)(2,1)} %w_ref.1, bf16[64,128,256]{2,1,0:T(8,128)(2,1)} %bitcast.1.src_ref), custom_call_target="tpu_custom_call" | custom-call | tf_op jit(solution)/shard_map/remap/pallas_call | solution.py:75
  81.4 32.0 %all_to_all.24 = bf16[8,32,4096]{2,1,0:T(8,128)(2,1)S(1)} all-to-all(bf16[8,32,4096]{2,1,0:T(8,128)(2,1)} %bitcast.7), channel_id=1, replica_groups=mesh['el'=8,'tg'=16] {'el'}, dimensions={0} | all-to-all | bytes 4194304 | tf_op jit(solution)/shard_map/all_to_all | solution.py:99
  113.3 1.5 %copy.9 = bf16[8,4,8,4096]{3,2,0,1:T(8,128)(2,1)} copy(bf16[8,4,8,4096]{3,2,1,0:T(8,128)(2,1)S(1)} %bitcast.8) | data formatting | bytes 4194304 | tf_op jit(solution)/shard_map/all_to_all | solution.py:99
Async XLA Ops:
  5.2 12.0 %copy-start = (s32[1,32,16]{1,2,0:T(8,128)S(1)}, s32[1,32,16]{1,2,0:T(8,128)}, u32[]{:S(2)}) copy-start(s32[1,32,16]{1,2,0:T(8,128)} %param.10) | copy-start | bytes 6148
  5.2 63.9 %all-to-all-start = ((bf16[128,64,256]{2,1,0:T(8,128)(2,1)}), bf16[128,64,256]{2,1,0:T(8,128)(2,1)}, u32[]{:S(2)}, u32[]{:S(2)}) async-start(bf16[128,64,256]{2,1,0:T(8,128)(2,1)} %bitcast.6), calls=%async_computation | async-start | bytes 8388608 | tf_op jit(solution)/shard_map/all_to_all | solution.py:96

commit v2 on v1

v2 whole, which is shorter than its diff:
```python
import functools

import jax
import jax.numpy as jnp
from jax import lax
from jax.experimental import pallas as pl
from jax.experimental.pallas import tpu as pltpu
from jax.sharding import PartitionSpec as P

PARTS = 2
HOPS = ((2, 0), (2, 1), (1, 0), (3, 0), (1, 1), (3, 1), (0, 1), (0, 0))


def pack_kernel(chunks, owner_ref, counts_ref, field_ref, out_ref, buf, dst, pos_v, pos_s, sem_in, sem_pos, sem_out):
    elems, points, channels = dst.shape
    step = elems // chunks
    owners = elems // 4

    def fetch(c):
        return pltpu.make_async_copy(field_ref.at[pl.ds(c * step, step)], buf.at[pl.ds(c * step, step)], sem_in.at[c])

    for c in range(chunks):
        fetch(c).start()
    owner = owner_ref[...]
    hit = lax.broadcasted_iota(jnp.int32, (owners, elems), 0) == owner
    hit = jnp.where(hit, 1.0, 0.0)
    before = jnp.where(lax.broadcasted_iota(jnp.int32, (elems, elems), 0) < lax.broadcasted_iota(jnp.int32, (elems, elems), 1), 1.0, 0.0)
    earlier = jnp.dot(hit.astype(jnp.bfloat16), before.astype(jnp.bfloat16), preferred_element_type=jnp.float32)
    rank = jnp.sum(hit * earlier, axis=0, keepdims=True)
    pos_v[...] = owner * 4 + rank.astype(jnp.int32)
    cp = pltpu.make_async_copy(pos_v, pos_s, sem_pos)
    cp.start()
    cp.wait()
    point = lax.broadcasted_iota(jnp.int32, (points, channels), 0)
    for c in range(chunks):
        fetch(c).wait()

        def body(e, carry):
            live = point < counts_ref[0, e]
            dst[pos_s[0, e]] = jnp.where(live, buf[e], jnp.zeros((), buf.dtype))
            return carry

        lax.fori_loop(c * step, (c + 1) * step, body, 0, unroll=8)
    out = pltpu.make_async_copy(dst, out_ref, sem_out)
    out.start()
    out.wait()


def pack(owner_map, send_counts, field, chunks=8):
    return pl.pallas_call(
        functools.partial(pack_kernel, chunks),
        out_shape=jax.ShapeDtypeStruct(field.shape, field.dtype),
        in_specs=[pl.BlockSpec(memory_space=pltpu.VMEM), pl.BlockSpec(memory_space=pltpu.SMEM), pl.BlockSpec(memory_space=pl.ANY)],
        out_specs=pl.BlockSpec(memory_space=pl.ANY),
        scratch_shapes=[
            pltpu.VMEM(field.shape, field.dtype),
            pltpu.VMEM(field.shape, field.dtype),
            pltpu.VMEM((1, field.shape[0]), jnp.int32),
            pltpu.SMEM((1, field.shape[0]), jnp.int32),
            pltpu.SemaphoreType.DMA((chunks,)),
            pltpu.SemaphoreType.DMA,
            pltpu.SemaphoreType.DMA,
        ],
        name="pack",
    )(owner_map, send_counts, field)


def peer(me, groups, hop):
    chip, core = me // 2, me % 2
    return lax.rem(chip + hop[0], groups // 2) * 2 + (1 - core if hop[1] else core)


def remap_kernel(part, lag, axis, rows_ref, cols_ref, w_ref, src_ref, *refs):
    outs, (w_buf, src, out, order, sem_src, sem_w) = refs[: len(HOPS)], refs[len(HOPS) :]
    _, targets, blocks, tile, _ = w_ref.shape
    count = w_buf.shape[0]
    me = lax.axis_index(axis) if axis else 0
    groups = len(HOPS)
    rows = out.shape[0] // groups
    load = pltpu.make_async_copy(src_ref, src, sem_src)
    load.start()
    for t in range(targets):
        order[rows_ref[0, t]] = t

    def fetch(q):
        return pltpu.make_async_copy(w_ref.at[0, order[part * count + q]], w_buf.at[q], sem_w.at[q])

    for q in range(count):
        fetch(q).start()
    load.wait()

    def body(s, carry):
        for u in range(lag):
            q = s * lag + u
            t = order[part * count + q]
            fetch(q).wait()
            w = jnp.concatenate([w_buf[q, k] for k in range(blocks)], axis=1)
            x = jnp.concatenate([src[cols_ref[0, t, k]] for k in range(blocks)], axis=0)
            r = jnp.dot(w, x, preferred_element_type=jnp.float32)
            out[:, pl.ds(pl.multiple_of(q * tile, tile), tile)] = r.T.astype(out.dtype)
        return carry

    lax.fori_loop(0, count // lag, body, 0)
    for i, hop in enumerate(HOPS):
        row = pl.multiple_of(peer(me, groups, hop) * rows, rows)
        outs[i][...] = out[pl.ds(row, rows)]


def remap(part, tile_rows, tile_cols, weights, source, lag=2, axis="el"):
    _, targets, blocks, tile, _ = weights.shape
    channels = source.shape[-1]
    count = targets // PARTS
    piece = jax.ShapeDtypeStruct((channels // len(HOPS), count * tile), source.dtype)
    return pl.pallas_call(
        functools.partial(remap_kernel, part, lag, axis),
        out_shape=[piece] * len(HOPS),
        in_specs=[pl.BlockSpec(memory_space=pltpu.SMEM)] * 2 + [pl.BlockSpec(memory_space=pl.ANY)] * 2,
        out_specs=[pl.BlockSpec(memory_space=pltpu.VMEM)] * len(HOPS),
        scratch_shapes=[
            pltpu.VMEM((count, *weights.shape[2:]), weights.dtype),
            pltpu.VMEM(source.shape, source.dtype),
            pltpu.VMEM((channels, count * tile), source.dtype),
            pltpu.SMEM((targets,), jnp.int32),
            pltpu.SemaphoreType.DMA,
            pltpu.SemaphoreType.DMA((count,)),
        ],
        compiler_params=pltpu.CompilerParams(vmem_limit_bytes=46 << 20),
        cost_estimate=pl.CostEstimate(
            flops=2 * count * blocks * tile * tile * channels,
            bytes_accessed=2 * (weights.size // PARTS + source.size),
            transcendentals=0,
        ),
    )(tile_rows, tile_cols, weights, source)


def join_kernel(part, axis, *refs):
    pieces, (out_ref, sems) = refs[: len(HOPS)], refs[-2:]
    me = lax.axis_index(axis) if axis else 0
    groups = len(HOPS)
    width = pieces[0].shape[1]
    stores = []
    for i, (chip, core) in enumerate(HOPS):
        source = peer(me, groups, ((groups // 2 - chip) % (groups // 2), core))
        lane = pl.multiple_of((source * PARTS + part) * width, width)
        stores.append(pltpu.make_async_copy(pieces[i], out_ref.at[:, pl.ds(lane, width)], sems.at[i]))
        stores[i].start()
    for store in stores:
        store.wait()


def join(part, pieces, whole=None, axis="el"):
    rows, width = pieces[0].shape
    groups = len(HOPS)
    kept = [] if whole is None else [whole]
    return pl.pallas_call(
        functools.partial(join_kernel, part, axis),
        out_shape=jax.ShapeDtypeStruct((rows, groups * PARTS * width), pieces[0].dtype),
        in_specs=[pl.BlockSpec(memory_space=pltpu.VMEM)] * groups + [pl.BlockSpec(memory_space=pl.ANY)] * len(kept),
        out_specs=pl.BlockSpec(memory_space=pl.ANY),
        scratch_shapes=[pltpu.SemaphoreType.DMA((groups,))],
        input_output_aliases={groups: 0} if kept else {},
        compiler_params=pltpu.CompilerParams(vmem_limit_bytes=8 << 20),
        cost_estimate=pl.CostEstimate(flops=0, bytes_accessed=4 * groups * rows * width, transcendentals=0),
    )(*pieces, *kept)


def on_device(field_points, owner_map, send_counts, tile_rows, tile_cols, weights):
    elems, points, channels = field_points.shape
    devices = lax.axis_size(("el", "tg"))
    groups = lax.axis_size("el")
    packed = pack(owner_map, send_counts, field_points)
    outgoing = packed.reshape(devices, elems // devices * points, channels)
    incoming = lax.all_to_all(outgoing, ("el", "tg"), split_axis=0, concat_axis=0, tiled=True)
    source = incoming.reshape(-1, weights.shape[-1], channels)
    whole = None
    for part in range(PARTS):
        pieces = remap(part, tile_rows, tile_cols, weights, source)
        received = []
        for piece, hop in zip(pieces, HOPS):
            if hop != (0, 0):
                pairs = [(i, (i // 2 + hop[0]) % (groups // 2) * 2 + (i + hop[1]) % 2) for i in range(groups)]
                piece = lax.ppermute(piece, "el", pairs)
            received.append(piece)
        whole = join(part, received, whole)
    return whole


def solution(mesh):
    return jax.shard_map(
        on_device,
        mesh=mesh,
        in_specs=(
            P(("el", "tg"), None, None),
            P(("el", "tg"), None),
            P(("el", "tg"), None),
            P(("el", "tg"), None),
            P(("el", "tg"), None, None),
            P(("el", "tg"), None, None, None, None),
        ),
        out_specs=P("el", "tg"),
        check_vma=False,
    )
```

time: 115 us -> 129 us (1.12)
  blocking collectives: 32 us -> 0 us
  Pallas kernels: 17.4 us -> 34.2 us
  waiting for transfers between devices: 51.2 us -> 66.9 us
  starting transfers between devices: 12 us -> 27.3 us
  local copies, waits for them, and re-layouts: 2.15 us -> 0.09 us
    all_to_all x1 -> x0, blocking collectives: 32 us -> none  [on_device(): return lax.all_to_all(merged, 'el', split_axis=0, concat_axis=1, tiled=True)]
    pallas_call x1 -> x4, Pallas kernels: 12.3 us -> 29.1 us  [the longest x2 27 us: remap(): pl.pallas_call(functools.partial(remap_kernel, part, lag, axis), out_shap...]
    ppermute x0 -> x14, starting transfers between devices: none -> 15.3 us  [on_device(): piece = lax.ppermute(piece, 'el', pairs)]
    ppermute x0 -> x14, waiting for transfers between devices: none -> 15.1 us  [on_device(): piece = lax.ppermute(piece, 'el', pairs)]
    all_to_all x1 -> x0, local copies, waits for them, and re-layouts: 1.45 us -> none  [on_device(): return lax.all_to_all(merged, 'el', split_axis=0, concat_axis=1, tiled=True)]
  transfers between devices with their start and end apart: 1 -> 15, of which waited for: 1 -> 7; matrix products, arithmetic and copies ran while one was open for 1% -> 0% of each run, Pallas kernels for 0% -> 11%
where the time goes in v2:
time: 129 us
  waiting for transfers between devices  66.9 us (52%)
  Pallas kernels  34.2 us (27%)
  starting transfers between devices  27.3 us (21%)
    all_to_all x1, waiting for transfers between devices, on_device(): lax.all_to_all(outgoing, ('el', 'tg'), split_axis=0, concat_axis=0, tiled...  51.9 us
    pallas_call x2, Pallas kernels, remap(): pl.pallas_call(functools.partial(remap_kernel, part, lag, axis), out_shap...  27 us
    ppermute x14, starting transfers between devices, on_device(): piece = lax.ppermute(piece, 'el', pairs)  15.3 us
    ppermute x14, waiting for transfers between devices, on_device(): piece = lax.ppermute(piece, 'el', pairs)  15.1 us
    all_to_all x1, starting transfers between devices, on_device(): lax.all_to_all(outgoing, ('el', 'tg'), split_axis=0, concat_axis=0, tiled...  12 us
    pallas_call x1, Pallas kernels, pack(): pl.pallas_call(functools.partial(pack_kernel, chunks), out_shape=jax.Shap...  5.16 us
  transfers between devices with their start and end apart: 15, of which 7 were waited for; matrix products, arithmetic and copies ran while one was open for 0% of the time, Pallas kernels for 11%

profile of v2, /device:TPU:1, one launch (start us, length us, event | category | flops | bytes accessed | tf_op | source)
XLA Modules:
  0.0 128.6 jit_solution(4359148328699332961)
XLA Ops:
  0.0 5.2 %pack.1 = bf16[512,16,256]{2,1,0:T(8,128)(2,1)} custom-call(s32[1,512]{1,0:T(1,128)} %owner_ref.1, s32[1,512]{1,0:T(1,128)} %counts_ref.1, bf16[512,16,256]{2,1,0:T(8,128)(2,1)} %field_ref.1), custom_call_target="tpu_custom_call" | custom-call | tf_op jit(solution)/shard_map/pack/pallas_call | solution.py:50
  5.2 12.0 %all-to-all-start = ((bf16[128,64,256]{2,1,0:T(8,128)(2,1)}), bf16[128,64,256]{2,1,0:T(8,128)(2,1)}, u32[]{:S(2)}, u32[]{:S(2)}) async-start(bf16[128,64,256]{2,1,0:T(8,128)(2,1)} %bitcast.2), calls=%async_computation | async-start | bytes 8388608 | tf_op jit(solution)/shard_map/all_to_all | solution.py:173
  17.2 0.1 copy.8.cols_ref
  17.2 51.9 %all-to-all-done = bf16[128,64,256]{2,1,0:T(8,128)(2,1)} async-done(((bf16[128,64,256]{2,1,0:T(8,128)(2,1)}), bf16[128,64,256]{2,1,0:T(8,128)(2,1)}, u32[]{:S(2)}, u32[]{:S(2)}) %all-to-all-start) | async-done | bytes 4194336 | tf_op jit(solution)/shard_map/all_to_all | solution.py:173
  69.1 13.5 %shard_map.65 = (bf16[32,2048]{1,0:T(8,128)(2,1)S(1)}, bf16[32,2048]{1,0:T(8,128)(2,1)S(1)}, bf16[32,2048]{1,0:T(8,128)(2,1)S(1)}, bf16[32,2048]{1,0:T(8,128)(2,...) custom-call(s32[1,32]{1,0:T(1,128)S(1)} %copy-done, ...), custom_call_target="tpu_custom_call" | custom-call | flops 2147483648 | bytes 12582912 | tf_op jit(solution)/shard_map/pallas_call | solution.py:114
  82.6 2.8 %collective-permute-start.10 = (bf16[32,2048]{1,0:T(8,128)(2,1)S(1)}, bf16[32,2048]{1,0:T(8,128)(2,1)S(1)}, u32[]{:S(2)}, u32[]{:S(2)}) collective-permute-start(bf16[32,2048]{1,0:T(8,128)(2,1)S(1)} %get-tuple-element.32), channel_id=1, source_target_pairs={{0,96},{16,112},{32,0},{48,16},{64,32},{80,48},{96,64},{112,80},{1... | collective-permute-start | bytes 393224 | tf_op jit(solution)/shard_map/ppermute | solution.py:182
  85.4 0.4 collective-permute-start.11
  85.8 2.6 %collective-permute-start.12 = (bf16[32,2048]{1,0:T(8,128)(2,1)S(1)}, bf16[32,2048]{1,0:T(8,128)(2,1)S(1)}, u32[]{:S(2)}, u32[]{:S(2)}) collective-permute-start(bf16[32,2048]{1,0:T(8,128)(2,1)S(1)} %get-tuple-element.34), channel_id=1, source_target_pairs={{0,112},{16,96},{32,16},{48,0},{64,48},{80,32},{96,80},{112,64},{1... | collective-permute-start | bytes 393224 | tf_op jit(solution)/shard_map/ppermute | solution.py:182
  88.3 1.9 %collective-permute-start.13 = (bf16[32,2048]{1,0:T(8,128)(2,1)S(1)}, bf16[32,2048]{1,0:T(8,128)(2,1)S(1)}, u32[]{:S(2)}, u32[]{:S(2)}) collective-permute-start(bf16[32,2048]{1,0:T(8,128)(2,1)S(1)} %get-tuple-element.35), channel_id=1, source_target_pairs={{0,16},{16,0},{32,48},{48,32},{64,80},{80,64},{96,112},{112,96},{1... | collective-permute-start | bytes 393224 | tf_op jit(solution)/shard_map/ppermute | solution.py:182
  90.2 13.5 %shard_map.64 = (bf16[32,2048]{1,0:T(8,128)(2,1)S(1)}, bf16[32,2048]{1,0:T(8,128)(2,1)S(1)}, bf16[32,2048]{1,0:T(8,128)(2,1)S(1)}, bf16[32,2048]{1,0:T(8,128)(2,...) custom-call(s32[1,32]{1,0:T(1,128)S(1)} %copy-done, ...), custom_call_target="tpu_custom_call" | custom-call | flops 2147483648 | bytes 12582912 | tf_op jit(solution)/shard_map/pallas_call | solution.py:114
  103.7 0.1 collective-permute-start.7
  103.8 3.1 %collective-permute-start.8 = (bf16[32,2048]{1,0:T(8,128)(2,1)S(1)}, bf16[32,2048]{1,0:T(8,128)(2,1)S(1)}, u32[]{:S(2)}, u32[]{:S(2)}) collective-permute-start(bf16[32,2048]{1,0:T(8,128)(2,1)S(1)} %get-tuple-element.30), channel_id=1, source_target_pairs={{0,80},{16,64},{32,112},{48,96},{64,16},{80,0},{96,48},{112,32},{1... | collective-permute-start | bytes 393224 | tf_op jit(solution)/shard_map/ppermute | solution.py:182
  106.9 1.3 %collective-permute-start = (bf16[32,2048]{1,0:T(8,128)(2,1)S(1)}, bf16[32,2048]{1,0:T(8,128)(2,1)S(1)}, u32[]{:S(2)}, u32[]{:S(2)}) collective-permute-start(bf16[32,2048]{1,0:T(8,128)(2,1)S(1)} %get-tuple-element.21), channel_id=1, source_target_pairs={{0,64},{16,80},{32,96},{48,112},{64,0},{80,16},{96,32},{112,48},{1... | collective-permute-start | bytes 393224 | tf_op jit(solution)/shard_map/ppermute | solution.py:182
  108.2 2.1 %collective-permute-start.1 = (bf16[32,2048]{1,0:T(8,128)(2,1)S(1)}, bf16[32,2048]{1,0:T(8,128)(2,1)S(1)}, u32[]{:S(2)}, u32[]{:S(2)}) collective-permute-start(bf16[32,2048]{1,0:T(8,128)(2,1)S(1)} %get-tuple-element.22), channel_id=1, source_target_pairs={{0,80},{16,64},{32,112},{48,96},{64,16},{80,0},{96,48},{112,32},{1... | collective-permute-start | bytes 393224 | tf_op jit(solution)/shard_map/ppermute | solution.py:182
  110.4 0.3 collective-permute-start.2
  110.7 3.2 %collective-permute-done.8.refs_1_ = bf16[32,2048]{1,0:T(8,128)(2,1)S(1)} collective-permute-done((bf16[32,2048]{1,0:T(8,128)(2,1)S(1)}, bf16[32,2048]{1,0:T(8,128)(2,1)S(1)}, u32[]{:S(2)}, u32[]{:S(2)}) %collective-permute-start.8) | collective-permute-done | bytes 131104 | tf_op jit(solution)/shard_map/ppermute | solution.py:182
  113.8 2.9 %collective-permute-done.9.refs_2_ = bf16[32,2048]{1,0:T(8,128)(2,1)S(1)} collective-permute-done((bf16[32,2048]{1,0:T(8,128)(2,1)S(1)}, bf16[32,2048]{1,0:T(8,128)(2,1)S(1)}, u32[]{:S(2)}, u32[]{:S(2)}) %collective-permute-start.9) | collective-permute-done | bytes 131104 | tf_op jit(solution)/shard_map/ppermute | solution.py:182
  116.7 2.1 %collective-permute-done.refs_0_ = bf16[32,2048]{1,0:T(8,128)(2,1)S(1)} collective-permute-done((bf16[32,2048]{1,0:T(8,128)(2,1)S(1)}, bf16[32,2048]{1,0:T(8,128)(2,1)S(1)}, u32[]{:S(2)}, u32[]{:S(2)}) %collective-permute-start) | collective-permute-done | bytes 131104 | tf_op jit(solution)/shard_map/ppermute | solution.py:182
  118.8 0.8 collective-permute-start.5
  119.6 2.6 %collective-permute-done.1.refs_1_ = bf16[32,2048]{1,0:T(8,128)(2,1)S(1)} collective-permute-done((bf16[32,2048]{1,0:T(8,128)(2,1)S(1)}, bf16[32,2048]{1,0:T(8,128)(2,1)S(1)}, u32[]{:S(2)}, u32[]{:S(2)}) %collective-permute-start.1) | collective-permute-done | bytes 131104 | tf_op jit(solution)/shard_map/ppermute | solution.py:182
  122.3 1.0 shard_map.66.refs_8_
  123.3 1.5 %collective-permute-done.2.refs_2_ = bf16[32,2048]{1,0:T(8,128)(2,1)S(1)} collective-permute-done((bf16[32,2048]{1,0:T(8,128)(2,1)S(1)}, bf16[32,2048]{1,0:T(8,128)(2,1)S(1)}, u32[]{:S(2)}, u32[]{:S(2)}) %collective-permute-start.2) | collective-permute-done | bytes 131104 | tf_op jit(solution)/shard_map/ppermute | solution.py:182
  124.8 2.8 %collective-permute-done.4.refs_4_ = bf16[32,2048]{1,0:T(8,128)(2,1)S(1)} collective-permute-done((bf16[32,2048]{1,0:T(8,128)(2,1)S(1)}, bf16[32,2048]{1,0:T(8,128)(2,1)S(1)}, u32[]{:S(2)}, u32[]{:S(2)}) %collective-permute-start.4) | collective-permute-done | bytes 131104 | tf_op jit(solution)/shard_map/ppermute | solution.py:182
  127.6 1.0 shard_map.67
  (16 shorter events, 0.0 us)
Async XLA Ops:
  5.2 12.0 %copy-start.1 = (s32[1,32,16]{1,2,0:T(8,128)S(1)}, s32[1,32,16]{1,2,0:T(8,128)}, u32[]{:S(2)}) copy-start(s32[1,32,16]{1,2,0:T(8,128)} %param.10) | copy-start | bytes 6148
  5.2 63.9 %copy-start = (s32[1,32]{1,0:T(1,128)S(1)}, s32[1,32]{1,0:T(1,128)}, u32[]{:S(2)}) copy-start(s32[1,32]{1,0:T(1,128)} %rows_ref.3) | copy-start | bytes 388
  5.2 63.9 %all-to-all-start = ((bf16[128,64,256]{2,1,0:T(8,128)(2,1)}), bf16[128,64,256]{2,1,0:T(8,128)(2,1)}, u32[]{:S(2)}, u32[]{:S(2)}) async-start(bf16[128,64,256]{2,1,0:T(8,128)(2,1)} %bitcast.2), calls=%async_computation | async-start | bytes 8388608 | tf_op jit(solution)/shard_map/all_to_all | solution.py:173
  82.6 21.2 %collective-permute-start.10 = (bf16[32,2048]{1,0:T(8,128)(2,1)S(1)}, bf16[32,2048]{1,0:T(8,128)(2,1)S(1)}, u32[]{:S(2)}, u32[]{:S(2)}) collective-permute-start(bf16[32,2048]{1,0:T(8,128)(2,1)S(1)} %get-tuple-element.32), channel_id=1, source_target_pairs={{0,96},{16,112},{32,0},{48,16},{64,32},{80,48},{96,64},{112,80},{1... | collective-permute-start | bytes 393224 | tf_op jit(solution)/shard_map/ppermute | solution.py:182
  85.4 21.5 %collective-permute-start.11 = (bf16[32,2048]{1,0:T(8,128)(2,1)S(1)}, bf16[32,2048]{1,0:T(8,128)(2,1)S(1)}, u32[]{:S(2)}, u32[]{:S(2)}) collective-permute-start(bf16[32,2048]{1,0:T(8,128)(2,1)S(1)} %get-tuple-element.33), channel_id=1, source_target_pairs={{0,48},{16,32},{32,80},{48,64},{64,112},{80,96},{96,16},{112,0},{1... | collective-permute-start | bytes 393224 | tf_op jit(solution)/shard_map/ppermute | solution.py:182
  85.8 21.2 %collective-permute-start.12 = (bf16[32,2048]{1,0:T(8,128)(2,1)S(1)}, bf16[32,2048]{1,0:T(8,128)(2,1)S(1)}, u32[]{:S(2)}, u32[]{:S(2)}) collective-permute-start(bf16[32,2048]{1,0:T(8,128)(2,1)S(1)} %get-tuple-element.34), channel_id=1, source_target_pairs={{0,112},{16,96},{32,16},{48,0},{64,48},{80,32},{96,80},{112,64},{1... | collective-permute-start | bytes 393224 | tf_op jit(solution)/shard_map/ppermute | solution.py:182
  88.3 19.9 %collective-permute-start.13 = (bf16[32,2048]{1,0:T(8,128)(2,1)S(1)}, bf16[32,2048]{1,0:T(8,128)(2,1)S(1)}, u32[]{:S(2)}, u32[]{:S(2)}) collective-permute-start(bf16[32,2048]{1,0:T(8,128)(2,1)S(1)} %get-tuple-element.35), channel_id=1, source_target_pairs={{0,16},{16,0},{32,48},{48,32},{64,80},{80,64},{96,112},{112,96},{1... | collective-permute-start | bytes 393224 | tf_op jit(solution)/shard_map/ppermute | solution.py:182
  103.7 6.7 %collective-permute-start.7 = (bf16[32,2048]{1,0:T(8,128)(2,1)S(1)}, bf16[32,2048]{1,0:T(8,128)(2,1)S(1)}, u32[]{:S(2)}, u32[]{:S(2)}) collective-permute-start(bf16[32,2048]{1,0:T(8,128)(2,1)S(1)} %get-tuple-element.29), channel_id=1, source_target_pairs={{0,64},{16,80},{32,96},{48,112},{64,0},{80,16},{96,32},{112,48},{1... | collective-permute-start | bytes 393224 | tf_op jit(solution)/shard_map/ppermute | solution.py:182
  103.8 10.0 %collective-permute-start.8 = (bf16[32,2048]{1,0:T(8,128)(2,1)S(1)}, bf16[32,2048]{1,0:T(8,128)(2,1)S(1)}, u32[]{:S(2)}, u32[]{:S(2)}) collective-permute-start(bf16[32,2048]{1,0:T(8,128)(2,1)S(1)} %get-tuple-element.30), channel_id=1, source_target_pairs={{0,80},{16,64},{32,112},{48,96},{64,16},{80,0},{96,48},{112,32},{1... | collective-permute-start | bytes 393224 | tf_op jit(solution)/shard_map/ppermute | solution.py:182
  106.9 9.8 %collective-permute-start.9 = (bf16[32,2048]{1,0:T(8,128)(2,1)S(1)}, bf16[32,2048]{1,0:T(8,128)(2,1)S(1)}, u32[]{:S(2)}, u32[]{:S(2)}) collective-permute-start(bf16[32,2048]{1,0:T(8,128)(2,1)S(1)} %get-tuple-element.31), channel_id=1, source_target_pairs={{0,32},{16,48},{32,64},{48,80},{64,96},{80,112},{96,0},{112,16},{1... | collective-permute-start | bytes 393224 | tf_op jit(solution)/shard_map/ppermute | solution.py:182
  106.9 11.9 %collective-permute-start = (bf16[32,2048]{1,0:T(8,128)(2,1)S(1)}, bf16[32,2048]{1,0:T(8,128)(2,1)S(1)}, u32[]{:S(2)}, u32[]{:S(2)}) collective-permute-start(bf16[32,2048]{1,0:T(8,128)(2,1)S(1)} %get-tuple-element.21), channel_id=1, source_target_pairs={{0,64},{16,80},{32,96},{48,112},{64,0},{80,16},{96,32},{112,48},{1... | collective-permute-start | bytes 393224 | tf_op jit(solution)/shard_map/ppermute | solution.py:182
  108.2 14.1 %collective-permute-start.1 = (bf16[32,2048]{1,0:T(8,128)(2,1)S(1)}, bf16[32,2048]{1,0:T(8,128)(2,1)S(1)}, u32[]{:S(2)}, u32[]{:S(2)}) collective-permute-start(bf16[32,2048]{1,0:T(8,128)(2,1)S(1)} %get-tuple-element.22), channel_id=1, source_target_pairs={{0,80},{16,64},{32,112},{48,96},{64,16},{80,0},{96,48},{112,32},{1... | collective-permute-start | bytes 393224 | tf_op jit(solution)/shard_map/ppermute | solution.py:182
  110.4 14.4 %collective-permute-start.2 = (bf16[32,2048]{1,0:T(8,128)(2,1)S(1)}, bf16[32,2048]{1,0:T(8,128)(2,1)S(1)}, u32[]{:S(2)}, u32[]{:S(2)}) collective-permute-start(bf16[32,2048]{1,0:T(8,128)(2,1)S(1)} %get-tuple-element.23), channel_id=1, source_target_pairs={{0,32},{16,48},{32,64},{48,80},{64,96},{80,112},{96,0},{112,16},{1... | collective-permute-start | bytes 393224 | tf_op jit(solution)/shard_map/ppermute | solution.py:182
  113.8 11.0 %collective-permute-start.3 = (bf16[32,2048]{1,0:T(8,128)(2,1)S(1)}, bf16[32,2048]{1,0:T(8,128)(2,1)S(1)}, u32[]{:S(2)}, u32[]{:S(2)}) collective-permute-start(bf16[32,2048]{1,0:T(8,128)(2,1)S(1)} %get-tuple-element.24), channel_id=1, source_target_pairs={{0,96},{16,112},{32,0},{48,16},{64,32},{80,48},{96,64},{112,80},{1... | collective-permute-start | bytes 393224 | tf_op jit(solution)/shard_map/ppermute | solution.py:182
  116.7 10.9 %collective-permute-start.4 = (bf16[32,2048]{1,0:T(8,128)(2,1)S(1)}, bf16[32,2048]{1,0:T(8,128)(2,1)S(1)}, u32[]{:S(2)}, u32[]{:S(2)}) collective-permute-start(bf16[32,2048]{1,0:T(8,128)(2,1)S(1)} %get-tuple-element.25), channel_id=1, source_target_pairs={{0,48},{16,32},{32,80},{48,64},{64,112},{80,96},{96,16},{112,0},{1... | collective-permute-start | bytes 393224 | tf_op jit(solution)/shard_map/ppermute | solution.py:182
  118.8 8.7 %collective-permute-start.5 = (bf16[32,2048]{1,0:T(8,128)(2,1)S(1)}, bf16[32,2048]{1,0:T(8,128)(2,1)S(1)}, u32[]{:S(2)}, u32[]{:S(2)}) collective-permute-start(bf16[32,2048]{1,0:T(8,128)(2,1)S(1)} %get-tuple-element.26), channel_id=1, source_target_pairs={{0,112},{16,96},{32,16},{48,0},{64,48},{80,32},{96,80},{112,64},{1... | collective-permute-start | bytes 393224 | tf_op jit(solution)/shard_map/ppermute | solution.py:182
  122.3 5.3 %collective-permute-start.6 = (bf16[32,2048]{1,0:T(8,128)(2,1)S(1)}, bf16[32,2048]{1,0:T(8,128)(2,1)S(1)}, u32[]{:S(2)}, u32[]{:S(2)}) collective-permute-start(bf16[32,2048]{1,0:T(8,128)(2,1)S(1)} %get-tuple-element.27), channel_id=1, source_target_pairs={{0,16},{16,0},{32,48},{48,32},{64,80},{80,64},{96,112},{112,96},{1... | collective-permute-start | bytes 393224 | tf_op jit(solution)/shard_map/ppermute | solution.py:182

commit v3 on v2

--- a/solution.py
+++ b/solution.py
@@ -7,7 +7,9 @@
 from jax.experimental.pallas import tpu as pltpu
 from jax.sharding import PartitionSpec as P
 
-PARTS = 2
+SHARES = (5, 3)
+GROUP = 4
+AHEAD = 2
 HOPS = ((2, 0), (2, 1), (1, 0), (3, 0), (1, 1), (3, 1), (0, 1), (0, 0))
 
 
@@ -15,10 +17,8 @@
     elems, points, channels = dst.shape
     step = elems // chunks
     owners = elems // 4
-
     def fetch(c):
         return pltpu.make_async_copy(field_ref.at[pl.ds(c * step, step)], buf.at[pl.ds(c * step, step)], sem_in.at[c])
-
     for c in range(chunks):
         fetch(c).start()
     owner = owner_ref[...]
@@ -34,12 +34,10 @@
     point = lax.broadcasted_iota(jnp.int32, (points, channels), 0)
     for c in range(chunks):
         fetch(c).wait()
-
         def body(e, carry):
             live = point < counts_ref[0, e]
             dst[pos_s[0, e]] = jnp.where(live, buf[e], jnp.zeros((), buf.dtype))
             return carry
-
         lax.fori_loop(c * step, (c + 1) * step, body, 0, unroll=8)
     out = pltpu.make_async_copy(dst, out_ref, sem_out)
     out.start()
@@ -70,11 +68,10 @@
     return lax.rem(chip + hop[0], groups // 2) * 2 + (1 - core if hop[1] else core)
 
 
-def remap_kernel(part, lag, axis, rows_ref, cols_ref, w_ref, src_ref, *refs):
+def remap_kernel(first, axis, rows_ref, cols_ref, w_ref, src_ref, *refs):
     outs, (w_buf, src, out, order, sem_src, sem_w) = refs[: len(HOPS)], refs[len(HOPS) :]
     _, targets, blocks, tile, _ = w_ref.shape
     count = w_buf.shape[0]
-    me = lax.axis_index(axis) if axis else 0
     groups = len(HOPS)
     rows = out.shape[0] // groups
     load = pltpu.make_async_copy(src_ref, src, sem_src)
@@ -83,36 +80,37 @@
         order[rows_ref[0, t]] = t
 
     def fetch(q):
-        return pltpu.make_async_copy(w_ref.at[0, order[part * count + q]], w_buf.at[q], sem_w.at[q])
-
-    for q in range(count):
+        return pltpu.make_async_copy(w_ref.at[0, order[first + q]], w_buf.at[q], sem_w.at[q])
+
+    for q in range(min(count, GROUP * AHEAD)):
         fetch(q).start()
     load.wait()
-
-    def body(s, carry):
-        for u in range(lag):
-            q = s * lag + u
-            t = order[part * count + q]
+    for g in range(0, count, GROUP):
+        for q in range(g, g + GROUP):
             fetch(q).wait()
-            w = jnp.concatenate([w_buf[q, k] for k in range(blocks)], axis=1)
-            x = jnp.concatenate([src[cols_ref[0, t, k]] for k in range(blocks)], axis=0)
-            r = jnp.dot(w, x, preferred_element_type=jnp.float32)
-            out[:, pl.ds(pl.multiple_of(q * tile, tile), tile)] = r.T.astype(out.dtype)
-        return carry
-
-    lax.fori_loop(0, count // lag, body, 0)
+        for q in range(g + GROUP * AHEAD, min(count, g + GROUP * AHEAD + GROUP)):
+            fetch(q).start()
+        for q in range(g, g + GROUP):
+            t = order[first + q]
+            total = None
+            for k in range(0, blocks, 2):
+                w = jnp.concatenate([w_buf[q, k], w_buf[q, k + 1]], axis=1)
+                x = jnp.concatenate([src[cols_ref[0, t, k]], src[cols_ref[0, t, k + 1]]], axis=0)
+                r = jnp.dot(w, x, preferred_element_type=jnp.float32)
+                total = r if total is None else total + r
+            out[:, q * tile : (q + 1) * tile] = total.T.astype(out.dtype)
+    me = lax.axis_index(axis) if axis else 0
     for i, hop in enumerate(HOPS):
         row = pl.multiple_of(peer(me, groups, hop) * rows, rows)
         outs[i][...] = out[pl.ds(row, rows)]
 
 
-def remap(part, tile_rows, tile_cols, weights, source, lag=2, axis="el"):
+def remap(first, count, tile_rows, tile_cols, weights, source, axis="el"):
     _, targets, blocks, tile, _ = weights.shape
     channels = source.shape[-1]
-    count = targets // PARTS
     piece = jax.ShapeDtypeStruct((channels // len(HOPS), count * tile), source.dtype)
     return pl.pallas_call(
-        functools.partial(remap_kernel, part, lag, axis),
+        functools.partial(remap_kernel, first, axis),
         out_shape=[piece] * len(HOPS),
         in_specs=[pl.BlockSpec(memory_space=pltpu.SMEM)] * 2 + [pl.BlockSpec(memory_space=pl.ANY)] * 2,
         out_specs=[pl.BlockSpec(memory_space=pltpu.VMEM)] * len(HOPS),
@@ -127,13 +125,13 @@
         compiler_params=pltpu.CompilerParams(vmem_limit_bytes=46 << 20),
         cost_estimate=pl.CostEstimate(
             flops=2 * count * blocks * tile * tile * channels,
-            bytes_accessed=2 * (weights.size // PARTS + source.size),
+            bytes_accessed=2 * (weights.size * count // targets + source.size),
             transcendentals=0,
         ),
     )(tile_rows, tile_cols, weights, source)
 
 
-def join_kernel(part, axis, *refs):
+def join_kernel(start, axis, *refs):
     pieces, (out_ref, sems) = refs[: len(HOPS)], refs[-2:]
     me = lax.axis_index(axis) if axis else 0
     groups = len(HOPS)
@@ -141,20 +139,20 @@
     stores = []
     for i, (chip, core) in enumerate(HOPS):
         source = peer(me, groups, ((groups // 2 - chip) % (groups // 2), core))
-        lane = pl.multiple_of((source * PARTS + part) * width, width)
+        lane = pl.multiple_of(source * (out_ref.shape[1] // groups) + start, 128)
         stores.append(pltpu.make_async_copy(pieces[i], out_ref.at[:, pl.ds(lane, width)], sems.at[i]))
         stores[i].start()
     for store in stores:
         store.wait()
 
 
-def join(part, pieces, whole=None, axis="el"):
+def join(start, span, pieces, whole=None, axis="el"):
     rows, width = pieces[0].shape
     groups = len(HOPS)
     kept = [] if whole is None else [whole]
     return pl.pallas_call(
-        functools.partial(join_kernel, part, axis),
-        out_shape=jax.ShapeDtypeStruct((rows, groups * PARTS * width), pieces[0].dtype),
+        functools.partial(join_kernel, start, axis),
+        out_shape=jax.ShapeDtypeStruct((rows, groups * span), pieces[0].dtype),
         in_specs=[pl.BlockSpec(memory_space=pltpu.VMEM)] * groups + [pl.BlockSpec(memory_space=pl.ANY)] * len(kept),
         out_specs=pl.BlockSpec(memory_space=pl.ANY),
         scratch_shapes=[pltpu.SemaphoreType.DMA((groups,))],
@@ -172,16 +170,19 @@
     outgoing = packed.reshape(devices, elems // devices * points, channels)
     incoming = lax.all_to_all(outgoing, ("el", "tg"), split_axis=0, concat_axis=0, tiled=True)
     source = incoming.reshape(-1, weights.shape[-1], channels)
-    whole = None
-    for part in range(PARTS):
-        pieces = remap(part, tile_rows, tile_cols, weights, source)
+    targets, tile = weights.shape[1], weights.shape[-1]
+    whole, first = None, 0
+    for share in SHARES:
+        count = targets * share // sum(SHARES)
+        pieces = remap(first, count, tile_rows, tile_cols, weights, source)
         received = []
         for piece, hop in zip(pieces, HOPS):
             if hop != (0, 0):
                 pairs = [(i, (i // 2 + hop[0]) % (groups // 2) * 2 + (i + hop[1]) % 2) for i in range(groups)]
                 piece = lax.ppermute(piece, "el", pairs)
             received.append(piece)
-        whole = join(part, received, whole)
+        whole = join(first * tile, targets * tile, received, whole)
+        first += count
     return whole
 
 

time: 129 us -> 117 us (0.907)
  Pallas kernels: 34.2 us -> 22.5 us
  waiting for transfers between devices: 66.9 us -> 60.7 us
  starting transfers between devices: 27.3 us -> 33.1 us
    pallas_call x4, Pallas kernels: 29.1 us -> 17.3 us  [the longest x2 15.3 us: remap(): pl.pallas_call(functools.partial(remap_kernel, first, axis), out_shape=[p...]
    ppermute x14, waiting for transfers between devices: 15.1 us -> 8.8 us  [on_device(): piece = lax.ppermute(piece, 'el', pairs)]
    ppermute x14, starting transfers between devices: 15.3 us -> 21.2 us  [on_device(): piece = lax.ppermute(piece, 'el', pairs)]
  transfers between devices with their start and end apart: 15 -> 15, of which waited for: 7 -> 7; matrix products, arithmetic and copies ran while one was open for 0% -> 0% of each run, Pallas kernels for 11% -> 7%
where the time goes in v3:
time: 117 us; the launch traced here: 116 us
  waiting for transfers between devices  60.7 us (52%)
  starting transfers between devices  33.1 us (28%)
  Pallas kernels  22.5 us (19%)
    all_to_all x1, waiting for transfers between devices, on_device(): lax.all_to_all(outgoing, ('el', 'tg'), split_axis=0, concat_axis=0, tiled...  51.9 us
    ppermute x14, starting transfers between devices, on_device(): piece = lax.ppermute(piece, 'el', pairs)  21.2 us
    pallas_call x2, Pallas kernels, remap(): pl.pallas_call(functools.partial(remap_kernel, first, axis), out_shape=[p...  15.3 us
    all_to_all x1, starting transfers between devices, on_device(): lax.all_to_all(outgoing, ('el', 'tg'), split_axis=0, concat_axis=0, tiled...  12 us
    ppermute x14, waiting for transfers between devices, on_device(): piece = lax.ppermute(piece, 'el', pairs)  8.8 us
    pallas_call x1, Pallas kernels, pack(): pl.pallas_call(functools.partial(pack_kernel, chunks), out_shape=jax.Shap...  5.16 us
  transfers between devices with their start and end apart: 15, of which 7 were waited for; matrix products, arithmetic and copies ran while one was open for 0% of the time, Pallas kernels for 7%

profile of v3, /device:TPU:1, one launch (start us, length us, event | category | flops | bytes accessed | tf_op | source)
XLA Modules:
  0.0 116.4 jit_solution(190007435217968384)
XLA Ops:
  0.0 5.2 %pack.1 = bf16[512,16,256]{2,1,0:T(8,128)(2,1)} custom-call(s32[1,512]{1,0:T(1,128)} %owner_ref.1, s32[1,512]{1,0:T(1,128)} %counts_ref.1, bf16[512,16,256]{2,1,0:T(8,128)(2,1)} %field_ref.1), custom_call_target="tpu_custom_call" | custom-call | tf_op jit(solution)/shard_map/pack/pallas_call | solution.py:48
  5.2 12.0 %all-to-all-start = ((bf16[128,64,256]{2,1,0:T(8,128)(2,1)}), bf16[128,64,256]{2,1,0:T(8,128)(2,1)}, u32[]{:S(2)}, u32[]{:S(2)}) async-start(bf16[128,64,256]{2,1,0:T(8,128)(2,1)} %bitcast.2), calls=%async_computation | async-start | bytes 8388608 | tf_op jit(solution)/shard_map/all_to_all | solution.py:171
  17.2 51.9 %all-to-all-done = bf16[128,64,256]{2,1,0:T(8,128)(2,1)} async-done(((bf16[128,64,256]{2,1,0:T(8,128)(2,1)}), bf16[128,64,256]{2,1,0:T(8,128)(2,1)}, u32[]{:S(2)}, u32[]{:S(2)}) %all-to-all-start) | async-done | bytes 4194336 | tf_op jit(solution)/shard_map/all_to_all | solution.py:171
  69.1 8.5 %shard_map.65 = (bf16[32,2560]{1,0:T(8,128)(2,1)S(1)}, bf16[32,2560]{1,0:T(8,128)(2,1)S(1)}, bf16[32,2560]{1,0:T(8,128)(2,1)S(1)}, bf16[32,2560]{1,0:T(8,128)(2,...) custom-call(s32[1,32]{1,0:T(1,128)S(1)} %copy-done, ...), custom_call_target="tpu_custom_call" | custom-call | flops 2684354560 | bytes 14680064 | tf_op jit(solution)/shard_map/pallas_call | solution.py:112
  77.6 2.8 %collective-permute-start.10 = (bf16[32,2560]{1,0:T(8,128)(2,1)S(1)}, bf16[32,2560]{1,0:T(8,128)(2,1)S(1)}, u32[]{:S(2)}, u32[]{:S(2)}) collective-permute-start(bf16[32,2560]{1,0:T(8,128)(2,1)S(1)} %get-tuple-element.32), channel_id=1, source_target_pairs={{0,96},{16,112},{32,0},{48,16},{64,32},{80,48},{96,64},{112,80},{1... | collective-permute-start | bytes 491528 | tf_op jit(solution)/shard_map/ppermute | solution.py:182
  80.8 6.8 %shard_map.64 = (bf16[32,1536]{1,0:T(8,128)(2,1)S(1)}, bf16[32,1536]{1,0:T(8,128)(2,1)S(1)}, bf16[32,1536]{1,0:T(8,128)(2,1)S(1)}, bf16[32,1536]{1,0:T(8,128)(2,...) custom-call(s32[1,32]{1,0:T(1,128)S(1)} %copy-done, ...), custom_call_target="tpu_custom_call" | custom-call | flops 1610612736 | bytes 10485760 | tf_op jit(solution)/shard_map/pallas_call | solution.py:112
  87.5 2.4 %collective-permute-start = (bf16[32,1536]{1,0:T(8,128)(2,1)S(1)}, bf16[32,1536]{1,0:T(8,128)(2,1)S(1)}, u32[]{:S(2)}, u32[]{:S(2)}) collective-permute-start(bf16[32,1536]{1,0:T(8,128)(2,1)S(1)} %get-tuple-element.21), channel_id=1, source_target_pairs={{0,64},{16,80},{32,96},{48,112},{64,0},{80,16},{96,32},{112,48},{1... | collective-permute-start | bytes 294920 | tf_op jit(solution)/shard_map/ppermute | solution.py:182
  90.0 2.3 %collective-permute-start.1 = (bf16[32,1536]{1,0:T(8,128)(2,1)S(1)}, bf16[32,1536]{1,0:T(8,128)(2,1)S(1)}, u32[]{:S(2)}, u32[]{:S(2)}) collective-permute-start(bf16[32,1536]{1,0:T(8,128)(2,1)S(1)} %get-tuple-element.22), channel_id=1, source_target_pairs={{0,80},{16,64},{32,112},{48,96},{64,16},{80,0},{96,48},{112,32},{1... | collective-permute-start | bytes 294920 | tf_op jit(solution)/shard_map/ppermute | solution.py:182
  92.2 2.7 %collective-permute-start.12 = (bf16[32,2560]{1,0:T(8,128)(2,1)S(1)}, bf16[32,2560]{1,0:T(8,128)(2,1)S(1)}, u32[]{:S(2)}, u32[]{:S(2)}) collective-permute-start(bf16[32,2560]{1,0:T(8,128)(2,1)S(1)} %get-tuple-element.34), channel_id=1, source_target_pairs={{0,112},{16,96},{32,16},{48,0},{64,48},{80,32},{96,80},{112,64},{1... | collective-permute-start | bytes 491528 | tf_op jit(solution)/shard_map/ppermute | solution.py:182
  94.9 1.3 %collective-permute-start.13 = (bf16[32,2560]{1,0:T(8,128)(2,1)S(1)}, bf16[32,2560]{1,0:T(8,128)(2,1)S(1)}, u32[]{:S(2)}, u32[]{:S(2)}) collective-permute-start(bf16[32,2560]{1,0:T(8,128)(2,1)S(1)} %get-tuple-element.35), channel_id=1, source_target_pairs={{0,16},{16,0},{32,48},{48,32},{64,80},{80,64},{96,112},{112,96},{1... | collective-permute-start | bytes 491528 | tf_op jit(solution)/shard_map/ppermute | solution.py:182
  96.6 1.3 %collective-permute-start.7 = (bf16[32,2560]{1,0:T(8,128)(2,1)S(1)}, bf16[32,2560]{1,0:T(8,128)(2,1)S(1)}, u32[]{:S(2)}, u32[]{:S(2)}) collective-permute-start(bf16[32,2560]{1,0:T(8,128)(2,1)S(1)} %get-tuple-element.29), channel_id=1, source_target_pairs={{0,64},{16,80},{32,96},{48,112},{64,0},{80,16},{96,32},{112,48},{1... | collective-permute-start | bytes 491528 | tf_op jit(solution)/shard_map/ppermute | solution.py:182
  97.9 1.5 %collective-permute-start.8 = (bf16[32,2560]{1,0:T(8,128)(2,1)S(1)}, bf16[32,2560]{1,0:T(8,128)(2,1)S(1)}, u32[]{:S(2)}, u32[]{:S(2)}) collective-permute-start(bf16[32,2560]{1,0:T(8,128)(2,1)S(1)} %get-tuple-element.30), channel_id=1, source_target_pairs={{0,80},{16,64},{32,112},{48,96},{64,16},{80,0},{96,48},{112,32},{1... | collective-permute-start | bytes 491528 | tf_op jit(solution)/shard_map/ppermute | solution.py:182
  99.3 1.3 %collective-permute-start.9 = (bf16[32,2560]{1,0:T(8,128)(2,1)S(1)}, bf16[32,2560]{1,0:T(8,128)(2,1)S(1)}, u32[]{:S(2)}, u32[]{:S(2)}) collective-permute-start(bf16[32,2560]{1,0:T(8,128)(2,1)S(1)} %get-tuple-element.31), channel_id=1, source_target_pairs={{0,32},{16,48},{32,64},{48,80},{64,96},{80,112},{96,0},{112,16},{1... | collective-permute-start | bytes 491528 | tf_op jit(solution)/shard_map/ppermute | solution.py:182
  100.6 0.8 collective-permute-start.2
  101.4 2.0 %collective-permute-start.3 = (bf16[32,1536]{1,0:T(8,128)(2,1)S(1)}, bf16[32,1536]{1,0:T(8,128)(2,1)S(1)}, u32[]{:S(2)}, u32[]{:S(2)}) collective-permute-start(bf16[32,1536]{1,0:T(8,128)(2,1)S(1)} %get-tuple-element.24), channel_id=1, source_target_pairs={{0,96},{16,112},{32,0},{48,16},{64,32},{80,48},{96,64},{112,80},{1... | collective-permute-start | bytes 294920 | tf_op jit(solution)/shard_map/ppermute | solution.py:182
  103.4 0.7 collective-permute-done.7.refs_0_
  104.2 1.3 %collective-permute-start.4 = (bf16[32,1536]{1,0:T(8,128)(2,1)S(1)}, bf16[32,1536]{1,0:T(8,128)(2,1)S(1)}, u32[]{:S(2)}, u32[]{:S(2)}) collective-permute-start(bf16[32,1536]{1,0:T(8,128)(2,1)S(1)} %get-tuple-element.25), channel_id=1, source_target_pairs={{0,48},{16,32},{32,80},{48,64},{64,112},{80,96},{96,16},{112,0},{1... | collective-permute-start | bytes 294920 | tf_op jit(solution)/shard_map/ppermute | solution.py:182
  105.5 2.3 %collective-permute-done.8.refs_1_ = bf16[32,2560]{1,0:T(8,128)(2,1)S(1)} collective-permute-done((bf16[32,2560]{1,0:T(8,128)(2,1)S(1)}, bf16[32,2560]{1,0:T(8,128)(2,1)S(1)}, u32[]{:S(2)}, u32[]{:S(2)}) %collective-permute-start.8) | collective-permute-done | bytes 163872 | tf_op jit(solution)/shard_map/ppermute | solution.py:182
  107.7 0.9 collective-permute-start.5
  108.6 2.7 %collective-permute-done.9.refs_2_ = bf16[32,2560]{1,0:T(8,128)(2,1)S(1)} collective-permute-done((bf16[32,2560]{1,0:T(8,128)(2,1)S(1)}, bf16[32,2560]{1,0:T(8,128)(2,1)S(1)}, u32[]{:S(2)}, u32[]{:S(2)}) %collective-permute-start.9) | collective-permute-done | bytes 163872 | tf_op jit(solution)/shard_map/ppermute | solution.py:182
  111.7 1.1 shard_map.66.refs_8_
  112.8 0.6 collective-permute-done.2.refs_2_
  113.4 2.1 %collective-permute-done.4.refs_4_ = bf16[32,1536]{1,0:T(8,128)(2,1)S(1)} collective-permute-done((bf16[32,1536]{1,0:T(8,128)(2,1)S(1)}, bf16[32,1536]{1,0:T(8,128)(2,1)S(1)}, u32[]{:S(2)}, u32[]{:S(2)}) %collective-permute-start.4) | collective-permute-done | bytes 98336 | tf_op jit(solution)/shard_map/ppermute | solution.py:182
  115.5 0.9 shard_map.67
  (16 shorter events, 1.2 us)
Async XLA Ops:
  5.2 12.0 %copy-start.1 = (s32[1,32,16]{1,2,0:T(8,128)S(1)}, s32[1,32,16]{1,2,0:T(8,128)}, u32[]{:S(2)}) copy-start(s32[1,32,16]{1,2,0:T(8,128)} %param.10) | copy-start | bytes 6148
  5.2 63.9 %copy-start = (s32[1,32]{1,0:T(1,128)S(1)}, s32[1,32]{1,0:T(1,128)}, u32[]{:S(2)}) copy-start(s32[1,32]{1,0:T(1,128)} %rows_ref.3) | copy-start | bytes 388
  5.2 63.9 %all-to-all-start = ((bf16[128,64,256]{2,1,0:T(8,128)(2,1)}), bf16[128,64,256]{2,1,0:T(8,128)(2,1)}, u32[]{:S(2)}, u32[]{:S(2)}) async-start(bf16[128,64,256]{2,1,0:T(8,128)(2,1)} %bitcast.2), calls=%async_computation | async-start | bytes 8388608 | tf_op jit(solution)/shard_map/all_to_all | solution.py:171
  77.6 20.2 %collective-permute-start.10 = (bf16[32,2560]{1,0:T(8,128)(2,1)S(1)}, bf16[32,2560]{1,0:T(8,128)(2,1)S(1)}, u32[]{:S(2)}, u32[]{:S(2)}) collective-permute-start(bf16[32,2560]{1,0:T(8,128)(2,1)S(1)} %get-tuple-element.32), channel_id=1, source_target_pairs={{0,96},{16,112},{32,0},{48,16},{64,32},{80,48},{96,64},{112,80},{1... | collective-permute-start | bytes 491528 | tf_op jit(solution)/shard_map/ppermute | solution.py:182
  80.4 19.0 %collective-permute-start.11 = (bf16[32,2560]{1,0:T(8,128)(2,1)S(1)}, bf16[32,2560]{1,0:T(8,128)(2,1)S(1)}, u32[]{:S(2)}, u32[]{:S(2)}) collective-permute-start(bf16[32,2560]{1,0:T(8,128)(2,1)S(1)} %get-tuple-element.33), channel_id=1, source_target_pairs={{0,48},{16,32},{32,80},{48,64},{64,112},{80,96},{96,16},{112,0},{1... | collective-permute-start | bytes 491528 | tf_op jit(solution)/shard_map/ppermute | solution.py:182
  87.5 7.4 %collective-permute-start = (bf16[32,1536]{1,0:T(8,128)(2,1)S(1)}, bf16[32,1536]{1,0:T(8,128)(2,1)S(1)}, u32[]{:S(2)}, u32[]{:S(2)}) collective-permute-start(bf16[32,1536]{1,0:T(8,128)(2,1)S(1)} %get-tuple-element.21), channel_id=1, source_target_pairs={{0,64},{16,80},{32,96},{48,112},{64,0},{80,16},{96,32},{112,48},{1... | collective-permute-start | bytes 294920 | tf_op jit(solution)/shard_map/ppermute | solution.py:182
  90.0 6.6 %collective-permute-start.1 = (bf16[32,1536]{1,0:T(8,128)(2,1)S(1)}, bf16[32,1536]{1,0:T(8,128)(2,1)S(1)}, u32[]{:S(2)}, u32[]{:S(2)}) collective-permute-start(bf16[32,1536]{1,0:T(8,128)(2,1)S(1)} %get-tuple-element.22), channel_id=1, source_target_pairs={{0,80},{16,64},{32,112},{48,96},{64,16},{80,0},{96,48},{112,32},{1... | collective-permute-start | bytes 294920 | tf_op jit(solution)/shard_map/ppermute | solution.py:182
  92.2 8.4 %collective-permute-start.12 = (bf16[32,2560]{1,0:T(8,128)(2,1)S(1)}, bf16[32,2560]{1,0:T(8,128)(2,1)S(1)}, u32[]{:S(2)}, u32[]{:S(2)}) collective-permute-start(bf16[32,2560]{1,0:T(8,128)(2,1)S(1)} %get-tuple-element.34), channel_id=1, source_target_pairs={{0,112},{16,96},{32,16},{48,0},{64,48},{80,32},{96,80},{112,64},{1... | collective-permute-start | bytes 491528 | tf_op jit(solution)/shard_map/ppermute | solution.py:182
  94.9 6.5 %collective-permute-start.13 = (bf16[32,2560]{1,0:T(8,128)(2,1)S(1)}, bf16[32,2560]{1,0:T(8,128)(2,1)S(1)}, u32[]{:S(2)}, u32[]{:S(2)}) collective-permute-start(bf16[32,2560]{1,0:T(8,128)(2,1)S(1)} %get-tuple-element.35), channel_id=1, source_target_pairs={{0,16},{16,0},{32,48},{48,32},{64,80},{80,64},{96,112},{112,96},{1... | collective-permute-start | bytes 491528 | tf_op jit(solution)/shard_map/ppermute | solution.py:182
  96.6 7.6 %collective-permute-start.7 = (bf16[32,2560]{1,0:T(8,128)(2,1)S(1)}, bf16[32,2560]{1,0:T(8,128)(2,1)S(1)}, u32[]{:S(2)}, u32[]{:S(2)}) collective-permute-start(bf16[32,2560]{1,0:T(8,128)(2,1)S(1)} %get-tuple-element.29), channel_id=1, source_target_pairs={{0,64},{16,80},{32,96},{48,112},{64,0},{80,16},{96,32},{112,48},{1... | collective-permute-start | bytes 491528 | tf_op jit(solution)/shard_map/ppermute | solution.py:182
  97.9 9.9 %collective-permute-start.8 = (bf16[32,2560]{1,0:T(8,128)(2,1)S(1)}, bf16[32,2560]{1,0:T(8,128)(2,1)S(1)}, u32[]{:S(2)}, u32[]{:S(2)}) collective-permute-start(bf16[32,2560]{1,0:T(8,128)(2,1)S(1)} %get-tuple-element.30), channel_id=1, source_target_pairs={{0,80},{16,64},{32,112},{48,96},{64,16},{80,0},{96,48},{112,32},{1... | collective-permute-start | bytes 491528 | tf_op jit(solution)/shard_map/ppermute | solution.py:182
  99.3 12.0 %collective-permute-start.9 = (bf16[32,2560]{1,0:T(8,128)(2,1)S(1)}, bf16[32,2560]{1,0:T(8,128)(2,1)S(1)}, u32[]{:S(2)}, u32[]{:S(2)}) collective-permute-start(bf16[32,2560]{1,0:T(8,128)(2,1)S(1)} %get-tuple-element.31), channel_id=1, source_target_pairs={{0,32},{16,48},{32,64},{48,80},{64,96},{80,112},{96,0},{112,16},{1... | collective-permute-start | bytes 491528 | tf_op jit(solution)/shard_map/ppermute | solution.py:182
  100.6 12.8 %collective-permute-start.2 = (bf16[32,1536]{1,0:T(8,128)(2,1)S(1)}, bf16[32,1536]{1,0:T(8,128)(2,1)S(1)}, u32[]{:S(2)}, u32[]{:S(2)}) collective-permute-start(bf16[32,1536]{1,0:T(8,128)(2,1)S(1)} %get-tuple-element.23), channel_id=1, source_target_pairs={{0,32},{16,48},{32,64},{48,80},{64,96},{80,112},{96,0},{112,16},{1... | collective-permute-start | bytes 294920 | tf_op jit(solution)/shard_map/ppermute | solution.py:182
  101.4 12.0 %collective-permute-start.3 = (bf16[32,1536]{1,0:T(8,128)(2,1)S(1)}, bf16[32,1536]{1,0:T(8,128)(2,1)S(1)}, u32[]{:S(2)}, u32[]{:S(2)}) collective-permute-start(bf16[32,1536]{1,0:T(8,128)(2,1)S(1)} %get-tuple-element.24), channel_id=1, source_target_pairs={{0,96},{16,112},{32,0},{48,16},{64,32},{80,48},{96,64},{112,80},{1... | collective-permute-start | bytes 294920 | tf_op jit(solution)/shard_map/ppermute | solution.py:182
  104.2 11.3 %collective-permute-start.4 = (bf16[32,1536]{1,0:T(8,128)(2,1)S(1)}, bf16[32,1536]{1,0:T(8,128)(2,1)S(1)}, u32[]{:S(2)}, u32[]{:S(2)}) collective-permute-start(bf16[32,1536]{1,0:T(8,128)(2,1)S(1)} %get-tuple-element.25), channel_id=1, source_target_pairs={{0,48},{16,32},{32,80},{48,64},{64,112},{80,96},{96,16},{112,0},{1... | collective-permute-start | bytes 294920 | tf_op jit(solution)/shard_map/ppermute | solution.py:182
  107.7 7.8 %collective-permute-start.5 = (bf16[32,1536]{1,0:T(8,128)(2,1)S(1)}, bf16[32,1536]{1,0:T(8,128)(2,1)S(1)}, u32[]{:S(2)}, u32[]{:S(2)}) collective-permute-start(bf16[32,1536]{1,0:T(8,128)(2,1)S(1)} %get-tuple-element.26), channel_id=1, source_target_pairs={{0,112},{16,96},{32,16},{48,0},{64,48},{80,32},{96,80},{112,64},{1... | collective-permute-start | bytes 294920 | tf_op jit(solution)/shard_map/ppermute | solution.py:182
  111.3 4.2 %collective-permute-start.6 = (bf16[32,1536]{1,0:T(8,128)(2,1)S(1)}, bf16[32,1536]{1,0:T(8,128)(2,1)S(1)}, u32[]{:S(2)}, u32[]{:S(2)}) collective-permute-start(bf16[32,1536]{1,0:T(8,128)(2,1)S(1)} %get-tuple-element.27), channel_id=1, source_target_pairs={{0,16},{16,0},{32,48},{48,32},{64,80},{80,64},{96,112},{112,96},{1... | collective-permute-start | bytes 294920 | tf_op jit(solution)/shard_map/ppermute | solution.py:182

commit v4 on v3

--- a/solution.py
+++ b/solution.py
@@ -7,7 +7,8 @@
 from jax.experimental.pallas import tpu as pltpu
 from jax.sharding import PartitionSpec as P
 
-SHARES = (5, 3)
+SHARES = (1, 1)
+CHIPS = (2, 1, 3, 0)
 GROUP = 4
 AHEAD = 2
 HOPS = ((2, 0), (2, 1), (1, 0), (3, 0), (1, 1), (3, 1), (0, 1), (0, 0))
@@ -63,13 +64,16 @@
     )(owner_map, send_counts, field)
 
 
+HOPS_OF = {False: HOPS, True: tuple((chip, 0) for chip in CHIPS)}
+
+
 def peer(me, groups, hop):
     chip, core = me // 2, me % 2
     return lax.rem(chip + hop[0], groups // 2) * 2 + (1 - core if hop[1] else core)
 
 
-def remap_kernel(first, axis, rows_ref, cols_ref, w_ref, src_ref, *refs):
-    outs, (w_buf, src, out, order, sem_src, sem_w) = refs[: len(HOPS)], refs[len(HOPS) :]
+def remap_kernel(first, paired, axis, rows_ref, cols_ref, w_ref, src_ref, *refs):
+    outs, (w_buf, src, out, order, sem_src, sem_w) = refs[:-6], refs[-6:]
     _, targets, blocks, tile, _ = w_ref.shape
     count = w_buf.shape[0]
     groups = len(HOPS)
@@ -100,20 +104,21 @@
                 total = r if total is None else total + r
             out[:, q * tile : (q + 1) * tile] = total.T.astype(out.dtype)
     me = lax.axis_index(axis) if axis else 0
-    for i, hop in enumerate(HOPS):
-        row = pl.multiple_of(peer(me, groups, hop) * rows, rows)
-        outs[i][...] = out[pl.ds(row, rows)]
-
-
-def remap(first, count, tile_rows, tile_cols, weights, source, axis="el"):
+    for piece, hop in zip(outs, HOPS_OF[paired]):
+        row = peer(me, groups, hop) // 2 * 2 if paired else peer(me, groups, hop)
+        piece[...] = out[pl.ds(pl.multiple_of(row * rows, rows), piece.shape[0])]
+
+
+def remap(first, count, paired, tile_rows, tile_cols, weights, source, axis="el"):
     _, targets, blocks, tile, _ = weights.shape
     channels = source.shape[-1]
-    piece = jax.ShapeDtypeStruct((channels // len(HOPS), count * tile), source.dtype)
-    return pl.pallas_call(
-        functools.partial(remap_kernel, first, axis),
-        out_shape=[piece] * len(HOPS),
+    pieces = len(HOPS_OF[paired])
+    piece = jax.ShapeDtypeStruct((channels // pieces, count * tile), source.dtype)
+    return pl.pallas_call(
+        functools.partial(remap_kernel, first, paired, axis),
+        out_shape=[piece] * pieces,
         in_specs=[pl.BlockSpec(memory_space=pltpu.SMEM)] * 2 + [pl.BlockSpec(memory_space=pl.ANY)] * 2,
-        out_specs=[pl.BlockSpec(memory_space=pltpu.VMEM)] * len(HOPS),
+        out_specs=[pl.BlockSpec(memory_space=pltpu.VMEM)] * pieces,
         scratch_shapes=[
             pltpu.VMEM((count, *weights.shape[2:]), weights.dtype),
             pltpu.VMEM(source.shape, source.dtype),
@@ -131,35 +136,77 @@
     )(tile_rows, tile_cols, weights, source)
 
 
-def join_kernel(start, axis, *refs):
-    pieces, (out_ref, sems) = refs[: len(HOPS)], refs[-2:]
+def place(me, groups, start, piece, hop, out_ref, sem):
+    chip, core = hop
+    source = peer(me, groups, ((groups // 2 - chip) % (groups // 2), core))
+    lane = pl.multiple_of(source * (out_ref.shape[1] // groups) + start, 128)
+    return pltpu.make_async_copy(piece, out_ref.at[:, pl.ds(lane, piece.shape[1])], sem)
+
+
+def join_kernel(start, groups, hops, axis, *refs):
+    out_ref, sems = refs[-2:]
     me = lax.axis_index(axis) if axis else 0
-    groups = len(HOPS)
-    width = pieces[0].shape[1]
+    rows = out_ref.shape[0]
     stores = []
-    for i, (chip, core) in enumerate(HOPS):
-        source = peer(me, groups, ((groups // 2 - chip) % (groups // 2), core))
-        lane = pl.multiple_of(source * (out_ref.shape[1] // groups) + start, 128)
-        stores.append(pltpu.make_async_copy(pieces[i], out_ref.at[:, pl.ds(lane, width)], sems.at[i]))
+    for i, hop in enumerate(hops):
+        piece = refs[i] if len(hops) == groups else refs[0].at[pl.ds(i * rows, rows)]
+        stores.append(place(me, groups, start, piece, hop, out_ref, sems.at[i]))
         stores[i].start()
     for store in stores:
         store.wait()
 
 
-def join(start, span, pieces, whole=None, axis="el"):
-    rows, width = pieces[0].shape
-    groups = len(HOPS)
-    kept = [] if whole is None else [whole]
-    return pl.pallas_call(
-        functools.partial(join_kernel, start, axis),
-        out_shape=jax.ShapeDtypeStruct((rows, groups * span), pieces[0].dtype),
-        in_specs=[pl.BlockSpec(memory_space=pltpu.VMEM)] * groups + [pl.BlockSpec(memory_space=pl.ANY)] * len(kept),
+def join(start, hops, groups, pieces, whole, axis="el"):
+    return pl.pallas_call(
+        functools.partial(join_kernel, start, groups, hops, axis),
+        out_shape=jax.ShapeDtypeStruct(whole.shape, whole.dtype),
+        in_specs=[pl.BlockSpec(memory_space=pltpu.VMEM)] * len(pieces) + [pl.BlockSpec(memory_space=pl.ANY)],
         out_specs=pl.BlockSpec(memory_space=pl.ANY),
-        scratch_shapes=[pltpu.SemaphoreType.DMA((groups,))],
-        input_output_aliases={groups: 0} if kept else {},
+        scratch_shapes=[pltpu.SemaphoreType.DMA((len(hops),))],
+        input_output_aliases={len(pieces): 0},
         compiler_params=pltpu.CompilerParams(vmem_limit_bytes=8 << 20),
-        cost_estimate=pl.CostEstimate(flops=0, bytes_accessed=4 * groups * rows * width, transcendentals=0),
-    )(*pieces, *kept)
+        cost_estimate=pl.CostEstimate(flops=0, bytes_accessed=4 * sum(p.size for p in pieces), transcendentals=0),
+    )(*pieces, whole)
+
+
+def split_kernel(start, groups, axis, *refs):
+    pieces, (out_ref, away_ref, sems) = refs[: len(CHIPS)], refs[-3:]
+    me = lax.axis_index(axis) if axis else 0
+    core = me % 2
+    rows = out_ref.shape[0]
+    stores = []
+    for i, chip in enumerate(CHIPS):
+        kept = pieces[i].at[pl.ds(pl.multiple_of(core * rows, rows), rows)]
+        stores.append(place(me, groups, start, kept, (chip, 0), out_ref, sems.at[i]))
+        stores[i].start()
+    for i in range(len(CHIPS)):
+        away_ref[i * rows : (i + 1) * rows] = pieces[i][pl.ds(pl.multiple_of((1 - core) * rows, rows), rows)]
+    for store in stores:
+        store.wait()
+
+
+def split(start, span, groups, pieces, axis="el"):
+    rows, width = pieces[0].shape[0] // 2, pieces[0].shape[1]
+    dtype = pieces[0].dtype
+    return pl.pallas_call(
+        functools.partial(split_kernel, start, groups, axis),
+        out_shape=[
+            jax.ShapeDtypeStruct((rows, groups * span), dtype),
+            jax.ShapeDtypeStruct((len(CHIPS) * rows, width), dtype),
+        ],
+        in_specs=[pl.BlockSpec(memory_space=pltpu.VMEM)] * len(pieces),
+        out_specs=[pl.BlockSpec(memory_space=pl.ANY), pl.BlockSpec(memory_space=pltpu.VMEM)],
+        scratch_shapes=[pltpu.SemaphoreType.DMA((len(CHIPS),))],
+        compiler_params=pltpu.CompilerParams(vmem_limit_bytes=8 << 20),
+        cost_estimate=pl.CostEstimate(flops=0, bytes_accessed=4 * sum(p.size for p in pieces), transcendentals=0),
+    )(*pieces)
+
+
+def send(piece, groups, hop):
+    if hop == (0, 0):
+        return piece
+    pairs = [(i, (i // 2 + hop[0]) % (groups // 2) * 2 + (i + hop[1]) % 2) for i in range(groups)]
+    return lax.ppermute(piece, "el", pairs)
 
 
 def on_device(field_points, owner_map, send_counts, tile_rows, tile_cols, weights):
@@ -171,18 +218,15 @@
     incoming = lax.all_to_all(outgoing, ("el", "tg"), split_axis=0, concat_axis=0, tiled=True)
     source = incoming.reshape(-1, weights.shape[-1], channels)
     targets, tile = weights.shape[1], weights.shape[-1]
-    whole, first = None, 0
-    for share in SHARES:
-        count = targets * share // sum(SHARES)
-        pieces = remap(first, count, tile_rows, tile_cols, weights, source)
-        received = []
-        for piece, hop in zip(pieces, HOPS):
-            if hop != (0, 0):
-                pairs = [(i, (i // 2 + hop[0]) % (groups // 2) * 2 + (i + hop[1]) % 2) for i in range(groups)]
-                piece = lax.ppermute(piece, "el", pairs)
-            received.append(piece)
-        whole = join(first * tile, targets * tile, received, whole)
-        first += count
+    count = targets * SHARES[0] // sum(SHARES)
+    pieces = remap(0, count, True, tile_rows, tile_cols, weights, source)
+    received = [send(piece, groups, hop) for piece, hop in zip(pieces, HOPS_OF[True])]
+    pieces = remap(count, targets - count, False, tile_rows, tile_cols, weights, source)
+    whole, away = split(0, targets * tile, groups, received)
+    away = send(away, groups, (0, 1))
+    received = [send(piece, groups, hop) for piece, hop in zip(pieces, HOPS)]
+    whole = join(0, tuple((chip, 1) for chip in CHIPS), groups, [away], whole)
+    whole = join(count * tile, HOPS, groups, received, whole)
     return whole
 
 

time: 117 us -> 118 us (level)
  waiting for transfers between devices: 60.7 us -> 64.9 us
  starting transfers between devices: 33.1 us -> 29.8 us
    ppermute x14 -> x11, waiting for transfers between devices: 8.8 us -> 13 us  [send(): return lax.ppermute(piece, 'el', pairs)]
    ppermute x14 -> x11, starting transfers between devices: 21.2 us -> 17.9 us  [send(): return lax.ppermute(piece, 'el', pairs)]
    pallas_call x4 -> x5, Pallas kernels: 17.3 us -> 18 us  [the longest x2 15.3 us: remap(): pl.pallas_call(functools.partial(remap_kernel, first, paired, axis), out_...]
  transfers between devices with their start and end apart: 15 -> 12, of which waited for: 7 -> 6; matrix products, arithmetic and copies ran while one was open for 0% -> 0% of each run, Pallas kernels for 7% -> 7%
where the time goes in v4:
time: 118 us
  waiting for transfers between devices  64.9 us (55%)
  starting transfers between devices  29.8 us (25%)
  Pallas kernels  23.1 us (20%)
    all_to_all x1, waiting for transfers between devices, on_device(): lax.all_to_all(outgoing, ('el', 'tg'), split_axis=0, concat_axis=0, tiled...  51.9 us
    ppermute x11, starting transfers between devices, send(): return lax.ppermute(piece, 'el', pairs)  17.9 us
    pallas_call x2, Pallas kernels, remap(): pl.pallas_call(functools.partial(remap_kernel, first, paired, axis), out_...  15.3 us
    ppermute x11, waiting for transfers between devices, send(): return lax.ppermute(piece, 'el', pairs)  13 us
    all_to_all x1, starting transfers between devices, on_device(): lax.all_to_all(outgoing, ('el', 'tg'), split_axis=0, concat_axis=0, tiled...  12 us
    pallas_call x1, Pallas kernels, pack(): pl.pallas_call(functools.partial(pack_kernel, chunks), out_shape=jax.Shap...  5.15 us
  transfers between devices with their start and end apart: 12, of which 6 were waited for; matrix products, arithmetic and copies ran while one was open for 0% of the time, Pallas kernels for 7%

profile of v4, /device:TPU:1, one launch (start us, length us, event | category | flops | bytes accessed | tf_op | source)
XLA Modules:
  0.0 118.0 jit_solution(13390551450470076638)
XLA Ops:
  0.0 5.1 %pack.1 = bf16[512,16,256]{2,1,0:T(8,128)(2,1)} custom-call(s32[1,512]{1,0:T(1,128)} %owner_ref.1, s32[1,512]{1,0:T(1,128)} %counts_ref.1, bf16[512,16,256]{2,1,0:T(8,128)(2,1)} %field_ref.1), custom_call_target="tpu_custom_call" | custom-call | tf_op jit(solution)/shard_map/pack/pallas_call | solution.py:49
  5.2 12.0 %all-to-all-start = ((bf16[128,64,256]{2,1,0:T(8,128)(2,1)}), bf16[128,64,256]{2,1,0:T(8,128)(2,1)}, u32[]{:S(2)}, u32[]{:S(2)}) async-start(bf16[128,64,256]{2,1,0:T(8,128)(2,1)} %bitcast.2), calls=%async_computation | async-start | bytes 8388608 | tf_op jit(solution)/shard_map/all_to_all | solution.py:218
  17.2 51.9 %all-to-all-done = bf16[128,64,256]{2,1,0:T(8,128)(2,1)} async-done(((bf16[128,64,256]{2,1,0:T(8,128)(2,1)}), bf16[128,64,256]{2,1,0:T(8,128)(2,1)}, u32[]{:S(2)}, u32[]{:S(2)}) %all-to-all-start) | async-done | bytes 4194336 | tf_op jit(solution)/shard_map/all_to_all | solution.py:218
  69.1 7.7 %shard_map.65 = (bf16[64,2048]{1,0:T(8,128)(2,1)S(1)}, bf16[64,2048]{1,0:T(8,128)(2,1)S(1)}, bf16[64,2048]{1,0:T(8,128)(2,1)S(1)}, bf16[64,2048]{1,0:T(8,128)(2,1)S(1)}) custom-call(s32[1,32]{1,0:T(1,128)S(1)} %copy-done, s32[1,32,16]{2,1,0:T(8,128)S(1)} %copy.9.cols_ref, bf16[1,32,16,128,128]{4,3,2,1,0:T(8,128)(2,1)} %w_ref.3, ...), custom_call_target="tpu_custom_call" | custom-call | flops 2147483648 | bytes 12582912 | tf_op jit(solution)/shard_map/pallas_call | solution.py:117
  76.8 3.0 %collective-permute-start.7 = (bf16[64,2048]{1,0:T(8,128)(2,1)S(1)}, bf16[64,2048]{1,0:T(8,128)(2,1)S(1)}, u32[]{:S(2)}, u32[]{:S(2)}) collective-permute-start(bf16[64,2048]{1,0:T(8,128)(2,1)S(1)} %get-tuple-element.27), channel_id=1, source_target_pairs={{0,64},{16,80},{32,96},{48,112},{64,0},{80,16},{96,32},{112,48},{1... | collective-permute-start | bytes 786440 | tf_op jit(solution)/shard_map/ppermute | solution.py:209
  79.8 0.3 collective-permute-start.8
  80.1 2.3 %collective-permute-start.9 = (bf16[64,2048]{1,0:T(8,128)(2,1)S(1)}, bf16[64,2048]{1,0:T(8,128)(2,1)S(1)}, u32[]{:S(2)}, u32[]{:S(2)}) collective-permute-start(bf16[64,2048]{1,0:T(8,128)(2,1)S(1)} %get-tuple-element.29), channel_id=1, source_target_pairs={{0,96},{16,112},{32,0},{48,16},{64,32},{80,48},{96,64},{112,80},{1... | collective-permute-start | bytes 786440 | tf_op jit(solution)/shard_map/ppermute | solution.py:209
  82.4 2.3 %collective-permute-done.7.refs_0_ = bf16[64,2048]{1,0:T(8,128)(2,1)S(1)} collective-permute-done((bf16[64,2048]{1,0:T(8,128)(2,1)S(1)}, bf16[64,2048]{1,0:T(8,128)(2,1)S(1)}, u32[]{:S(2)}, u32[]{:S(2)}) %collective-permute-start.7) | collective-permute-done | bytes 262176 | tf_op jit(solution)/shard_map/ppermute | solution.py:209
  84.8 7.3 %collective-permute-done.8.refs_1_ = bf16[64,2048]{1,0:T(8,128)(2,1)S(1)} collective-permute-done((bf16[64,2048]{1,0:T(8,128)(2,1)S(1)}, bf16[64,2048]{1,0:T(8,128)(2,1)S(1)}, u32[]{:S(2)}, u32[]{:S(2)}) %collective-permute-start.8) | collective-permute-done | bytes 262176 | tf_op jit(solution)/shard_map/ppermute | solution.py:209
  92.0 0.8 shard_map.66
  92.9 1.0 collective-permute-start.10
  93.9 7.7 %shard_map.64 = (bf16[32,2048]{1,0:T(8,128)(2,1)S(1)}, bf16[32,2048]{1,0:T(8,128)(2,1)S(1)}, bf16[32,2048]{1,0:T(8,128)(2,1)S(1)}, bf16[32,2048]{1,0:T(8,128)(2,...) custom-call(s32[1,32]{1,0:T(1,128)S(1)} %copy-done, ...), custom_call_target="tpu_custom_call" | custom-call | flops 2147483648 | bytes 12582912 | tf_op jit(solution)/shard_map/pallas_call | solution.py:117
  101.6 1.9 %collective-permute-start = (bf16[32,2048]{1,0:T(8,128)(2,1)S(1)}, bf16[32,2048]{1,0:T(8,128)(2,1)S(1)}, u32[]{:S(2)}, u32[]{:S(2)}) collective-permute-start(bf16[32,2048]{1,0:T(8,128)(2,1)S(1)} %get-tuple-element.19), channel_id=1, source_target_pairs={{0,64},{16,80},{32,96},{48,112},{64,0},{80,16},{96,32},{112,48},{1... | collective-permute-start | bytes 393224 | tf_op jit(solution)/shard_map/ppermute | solution.py:209
  103.4 1.4 %collective-permute-start.1 = (bf16[32,2048]{1,0:T(8,128)(2,1)S(1)}, bf16[32,2048]{1,0:T(8,128)(2,1)S(1)}, u32[]{:S(2)}, u32[]{:S(2)}) collective-permute-start(bf16[32,2048]{1,0:T(8,128)(2,1)S(1)} %get-tuple-element.20), channel_id=1, source_target_pairs={{0,80},{16,64},{32,112},{48,96},{64,16},{80,0},{96,48},{112,32},{1... | collective-permute-start | bytes 393224 | tf_op jit(solution)/shard_map/ppermute | solution.py:209
  104.8 1.2 collective-permute-start.2
  106.0 1.5 %collective-permute-start.3 = (bf16[32,2048]{1,0:T(8,128)(2,1)S(1)}, bf16[32,2048]{1,0:T(8,128)(2,1)S(1)}, u32[]{:S(2)}, u32[]{:S(2)}) collective-permute-start(bf16[32,2048]{1,0:T(8,128)(2,1)S(1)} %get-tuple-element.22), channel_id=1, source_target_pairs={{0,96},{16,112},{32,0},{48,16},{64,32},{80,48},{96,64},{112,80},{1... | collective-permute-start | bytes 393224 | tf_op jit(solution)/shard_map/ppermute | solution.py:209
  107.5 0.7 collective-permute-done.refs_0_
  108.2 2.5 %collective-permute-start.4 = (bf16[32,2048]{1,0:T(8,128)(2,1)S(1)}, bf16[32,2048]{1,0:T(8,128)(2,1)S(1)}, u32[]{:S(2)}, u32[]{:S(2)}) collective-permute-start(bf16[32,2048]{1,0:T(8,128)(2,1)S(1)} %get-tuple-element.23), channel_id=1, source_target_pairs={{0,48},{16,32},{32,80},{48,64},{64,112},{80,96},{96,16},{112,0},{1... | collective-permute-start | bytes 393224 | tf_op jit(solution)/shard_map/ppermute | solution.py:209
  110.7 1.0 collective-permute-done.1.refs_1_
  111.7 2.1 %collective-permute-start.5 = (bf16[32,2048]{1,0:T(8,128)(2,1)S(1)}, bf16[32,2048]{1,0:T(8,128)(2,1)S(1)}, u32[]{:S(2)}, u32[]{:S(2)}) collective-permute-start(bf16[32,2048]{1,0:T(8,128)(2,1)S(1)} %get-tuple-element.24), channel_id=1, source_target_pairs={{0,112},{16,96},{32,16},{48,0},{64,48},{80,32},{96,80},{112,64},{1... | collective-permute-start | bytes 393224 | tf_op jit(solution)/shard_map/ppermute | solution.py:209
  113.8 0.7 collective-permute-start.6
  114.5 0.8 shard_map.67.refs_8_
  115.3 1.7 %collective-permute-done.4.refs_4_ = bf16[32,2048]{1,0:T(8,128)(2,1)S(1)} collective-permute-done((bf16[32,2048]{1,0:T(8,128)(2,1)S(1)}, bf16[32,2048]{1,0:T(8,128)(2,1)S(1)}, u32[]{:S(2)}, u32[]{:S(2)}) %collective-permute-start.4) | collective-permute-done | bytes 131104 | tf_op jit(solution)/shard_map/ppermute | solution.py:209
  117.0 1.0 shard_map.68
  (11 shorter events, 0.1 us)
Async XLA Ops:
  5.2 12.0 %copy-start.1 = (s32[1,32,16]{1,2,0:T(8,128)S(1)}, s32[1,32,16]{1,2,0:T(8,128)}, u32[]{:S(2)}) copy-start(s32[1,32,16]{1,2,0:T(8,128)} %param.10) | copy-start | bytes 6148
  5.2 63.9 %copy-start = (s32[1,32]{1,0:T(1,128)S(1)}, s32[1,32]{1,0:T(1,128)}, u32[]{:S(2)}) copy-start(s32[1,32]{1,0:T(1,128)} %rows_ref.3) | copy-start | bytes 388
  5.2 63.9 %all-to-all-start = ((bf16[128,64,256]{2,1,0:T(8,128)(2,1)}), bf16[128,64,256]{2,1,0:T(8,128)(2,1)}, u32[]{:S(2)}, u32[]{:S(2)}) async-start(bf16[128,64,256]{2,1,0:T(8,128)(2,1)} %bitcast.2), calls=%async_computation | async-start | bytes 8388608 | tf_op jit(solution)/shard_map/all_to_all | solution.py:218
  76.8 8.0 %collective-permute-start.7 = (bf16[64,2048]{1,0:T(8,128)(2,1)S(1)}, bf16[64,2048]{1,0:T(8,128)(2,1)S(1)}, u32[]{:S(2)}, u32[]{:S(2)}) collective-permute-start(bf16[64,2048]{1,0:T(8,128)(2,1)S(1)} %get-tuple-element.27), channel_id=1, source_target_pairs={{0,64},{16,80},{32,96},{48,112},{64,0},{80,16},{96,32},{112,48},{1... | collective-permute-start | bytes 786440 | tf_op jit(solution)/shard_map/ppermute | solution.py:209
  79.8 12.3 %collective-permute-start.8 = (bf16[64,2048]{1,0:T(8,128)(2,1)S(1)}, bf16[64,2048]{1,0:T(8,128)(2,1)S(1)}, u32[]{:S(2)}, u32[]{:S(2)}) collective-permute-start(bf16[64,2048]{1,0:T(8,128)(2,1)S(1)} %get-tuple-element.28), channel_id=1, source_target_pairs={{0,32},{16,48},{32,64},{48,80},{64,96},{80,112},{96,0},{112,16},{1... | collective-permute-start | bytes 786440 | tf_op jit(solution)/shard_map/ppermute | solution.py:209
  80.1 11.9 %collective-permute-start.9 = (bf16[64,2048]{1,0:T(8,128)(2,1)S(1)}, bf16[64,2048]{1,0:T(8,128)(2,1)S(1)}, u32[]{:S(2)}, u32[]{:S(2)}) collective-permute-start(bf16[64,2048]{1,0:T(8,128)(2,1)S(1)} %get-tuple-element.29), channel_id=1, source_target_pairs={{0,96},{16,112},{32,0},{48,16},{64,32},{80,48},{96,64},{112,80},{1... | collective-permute-start | bytes 786440 | tf_op jit(solution)/shard_map/ppermute | solution.py:209
  92.9 20.9 %collective-permute-start.10 = (bf16[128,2048]{1,0:T(8,128)(2,1)S(1)}, bf16[128,2048]{1,0:T(8,128)(2,1)S(1)}, u32[]{:S(2)}, u32[]{:S(2)}) collective-permute-start(bf16[128,2048]{1,0:T(8,128)(2,1)S(1)} %get-tuple-element.31), channel_id=1, source_target_pairs={{0,16},{16,0},{32,48},{48,32},{64,80},{80,64},{96,112},{112,96},{1... | collective-permute-start | bytes 1572872 | tf_op jit(solution)/shard_map/ppermute | solution.py:209
  101.6 6.6 %collective-permute-start = (bf16[32,2048]{1,0:T(8,128)(2,1)S(1)}, bf16[32,2048]{1,0:T(8,128)(2,1)S(1)}, u32[]{:S(2)}, u32[]{:S(2)}) collective-permute-start(bf16[32,2048]{1,0:T(8,128)(2,1)S(1)} %get-tuple-element.19), channel_id=1, source_target_pairs={{0,64},{16,80},{32,96},{48,112},{64,0},{80,16},{96,32},{112,48},{1... | collective-permute-start | bytes 393224 | tf_op jit(solution)/shard_map/ppermute | solution.py:209
  103.4 8.3 %collective-permute-start.1 = (bf16[32,2048]{1,0:T(8,128)(2,1)S(1)}, bf16[32,2048]{1,0:T(8,128)(2,1)S(1)}, u32[]{:S(2)}, u32[]{:S(2)}) collective-permute-start(bf16[32,2048]{1,0:T(8,128)(2,1)S(1)} %get-tuple-element.20), channel_id=1, source_target_pairs={{0,80},{16,64},{32,112},{48,96},{64,16},{80,0},{96,48},{112,32},{1... | collective-permute-start | bytes 393224 | tf_op jit(solution)/shard_map/ppermute | solution.py:209
  104.8 10.5 %collective-permute-start.2 = (bf16[32,2048]{1,0:T(8,128)(2,1)S(1)}, bf16[32,2048]{1,0:T(8,128)(2,1)S(1)}, u32[]{:S(2)}, u32[]{:S(2)}) collective-permute-start(bf16[32,2048]{1,0:T(8,128)(2,1)S(1)} %get-tuple-element.21), channel_id=1, source_target_pairs={{0,32},{16,48},{32,64},{48,80},{64,96},{80,112},{96,0},{112,16},{1... | collective-permute-start | bytes 393224 | tf_op jit(solution)/shard_map/ppermute | solution.py:209
  106.0 9.4 %collective-permute-start.3 = (bf16[32,2048]{1,0:T(8,128)(2,1)S(1)}, bf16[32,2048]{1,0:T(8,128)(2,1)S(1)}, u32[]{:S(2)}, u32[]{:S(2)}) collective-permute-start(bf16[32,2048]{1,0:T(8,128)(2,1)S(1)} %get-tuple-element.22), channel_id=1, source_target_pairs={{0,96},{16,112},{32,0},{48,16},{64,32},{80,48},{96,64},{112,80},{1... | collective-permute-start | bytes 393224 | tf_op jit(solution)/shard_map/ppermute | solution.py:209
  108.2 8.8 %collective-permute-start.4 = (bf16[32,2048]{1,0:T(8,128)(2,1)S(1)}, bf16[32,2048]{1,0:T(8,128)(2,1)S(1)}, u32[]{:S(2)}, u32[]{:S(2)}) collective-permute-start(bf16[32,2048]{1,0:T(8,128)(2,1)S(1)} %get-tuple-element.23), channel_id=1, source_target_pairs={{0,48},{16,32},{32,80},{48,64},{64,112},{80,96},{96,16},{112,0},{1... | collective-permute-start | bytes 393224 | tf_op jit(solution)/shard_map/ppermute | solution.py:209
  111.7 5.3 %collective-permute-start.5 = (bf16[32,2048]{1,0:T(8,128)(2,1)S(1)}, bf16[32,2048]{1,0:T(8,128)(2,1)S(1)}, u32[]{:S(2)}, u32[]{:S(2)}) collective-permute-start(bf16[32,2048]{1,0:T(8,128)(2,1)S(1)} %get-tuple-element.24), channel_id=1, source_target_pairs={{0,112},{16,96},{32,16},{48,0},{64,48},{80,32},{96,80},{112,64},{1... | collective-permute-start | bytes 393224 | tf_op jit(solution)/shard_map/ppermute | solution.py:209
  113.8 3.3 %collective-permute-start.6 = (bf16[32,2048]{1,0:T(8,128)(2,1)S(1)}, bf16[32,2048]{1,0:T(8,128)(2,1)S(1)}, u32[]{:S(2)}, u32[]{:S(2)}) collective-permute-start(bf16[32,2048]{1,0:T(8,128)(2,1)S(1)} %get-tuple-element.25), channel_id=1, source_target_pairs={{0,16},{16,0},{32,48},{48,32},{64,80},{80,64},{96,112},{112,96},{1... | collective-permute-start | bytes 393224 | tf_op jit(solution)/shard_map/ppermute | solution.py:209
